TPU v7x, 128 devices: a whole 4x4x4 slice. The times are simulated.
128 devices in a mesh: sy: 8 (over x_hi, z), sx: 16 (over y, x_lo, core).
Axes of the slice: x: 4 (x_hi: 2, x_lo: 2; x = x_hi * 2 + x_lo), y: 4, z: 4, core: 2. Of those that a mesh axis runs over, the one named last changes fastest.
Arguments:
- exposures: bfloat16 [4, 8, 512, 8192], P(None, None, 'sy', 'sx'), may hold values from -6 to 6
- psf_kernels: bfloat16 [4, 8, 21, 21], replicated, may hold values from -0.25 to 0.25
- clip_masks: int32 [4, 8, 512, 8192], P(None, None, 'sy', 'sx'), may hold values from 0 to 255
- exposure_weights: float32 [4, 8], replicated, may hold values from 0.5 to 2
- plane_offsets: int32 [3, 8, 2], replicated, may hold values from -384 to 384, as said below
- start_flux: float32 [8, 512, 8192], P(None, 'sy', 'sx'), may hold values from -6 to 6
- start_weight: float32 [8, 512, 8192], P(None, 'sy', 'sx'), may hold values from 1 to 4
Outputs:
- stacked_flux: float32 [8, 512, 8192], P(None, 'sy', 'sx')
- stacked_weight: float32 [8, 512, 8192], P(None, 'sy', 'sx')
Inputs may be any that keep to these rules, and one draw needn't show every extreme that they name: `clip_masks`: bit p of an entry is 1 where plane p clips that pixel of that exposure. plane_offsets[n, p, 0] moves rows and plane_offsets[n, p, 1] moves columns; a row offset has magnitude 64 // 4 to 48, positive for p < 4 and negative otherwise; a column offset has magnitude 512 // 4 to 384, positive for even p and negative for odd p; in every draw some row offset of each sign has magnitude 3 * 16 and some column offset of each sign has magnitude 3 * 128.
All inputs are finite; a program needn't handle non-finite values.
Results may differ from a plain program's by a relative error of at most 0.0003.
Values may be sent and summed in bfloat16 or wider, within the bound.
A program may use at most 128 MiB of HBM per device.

v0:
```python
import jax
import jax.numpy as jnp
from jax import lax
from jax.sharding import PartitionSpec as P

band_scale = 1.5
weight_floor = 1.0


def from_behind(value, axis, steps):
    count = lax.axis_size(axis)
    initial, last = (max(0, -steps), min(count, count - steps))
    return lax.ppermute(value, axis, [(source, source + steps) for source in range(initial, last)])


def padded_2(cells, sides, width):
    for axis, dim in sides:
        count = lax.axis_size(axis)
        ends = count - 1
        head = lax.slice_in_dim(cells, 0, width, axis=dim)
        tail = lax.slice_in_dim(cells, cells.shape[dim] - width, cells.shape[dim], axis=dim)
        cells = jnp.concatenate(
            [
                lax.ppermute(tail, axis, [(i, (i + 1) % count) for i in range(ends)]),
                cells,
                lax.ppermute(head, axis, [((i + 1) % count, i) for i in range(ends)]),
            ],
            axis=dim,
        )
    return cells


def tap_selector(kernel_size, tile_rows):
    table_shape = (kernel_size, tile_rows, tile_rows + kernel_size - 1)
    tap_index = lax.broadcasted_iota(jnp.int32, table_shape, 0)
    output_row = lax.broadcasted_iota(jnp.int32, table_shape, 1)
    source_row = lax.broadcasted_iota(jnp.int32, table_shape, 2)
    return (source_row - output_row == tap_index).astype(jnp.bfloat16)


def filter_tile(padded, kernel, selector):
    kernel_size = kernel.shape[0]
    tile_cols = padded.shape[1] - kernel_size + 1
    banded = jnp.einsum("ab,air->bir", kernel, selector, preferred_element_type=jnp.float32).astype(
        jnp.bfloat16
    )
    windows = jnp.stack(
        [padded[:, column_tap : column_tap + tile_cols] for column_tap in range(kernel_size)]
    )
    return jnp.einsum("bir,brj->ij", banded, windows, preferred_element_type=jnp.float32)


def accumulate(stacks, filtered, clip_mask, weight_value, powers):
    flux_stack = stacks[:, 0]
    weight_stack = stacks[:, 1]
    clip_bits = clip_mask[None] // powers[:, None, None] % 2
    running_mean = flux_stack / jnp.maximum(weight_stack, weight_floor)
    band_half = band_scale / jnp.sqrt(weight_value)
    clipped = jnp.clip(filtered[None], running_mean - band_half, running_mean + band_half)
    chosen = jnp.where(clip_bits == 1, clipped, filtered[None])
    return jnp.stack([flux_stack + weight_value * chosen, weight_stack + weight_value], axis=1)


def take_window(blocks, starts, length, axis_number):

    def window_one(single, first_cell):
        return lax.dynamic_slice_in_dim(single, first_cell, length, axis_number - 1)

    return jax.vmap(window_one)(blocks, starts)


def shift_rows(stacks, row_offsets):
    tile_rows = stacks.shape[2]
    margin = 3 * tile_rows // 4
    half_planes = stacks.shape[0] // 2
    downward = stacks[:half_planes]
    upward = stacks[half_planes:]
    from_above = from_behind(downward[:, :, tile_rows - margin :, :], "sy", 1)
    from_below = from_behind(upward[:, :, :margin, :], "sy", -1)
    extended_down = jnp.concatenate([from_above, downward], axis=2)
    extended_up = jnp.concatenate([upward, from_below], axis=2)
    moved_down = take_window(extended_down, margin - row_offsets[:half_planes], tile_rows, 2)
    moved_up = take_window(extended_up, -row_offsets[half_planes:], tile_rows, 2)
    return jnp.concatenate([moved_down, moved_up], axis=0)


def shift_columns(stacks, column_offsets):
    planes_total, pair_count, tile_rows, tile_cols = stacks.shape
    margin = 3 * tile_cols // 4
    grouped = stacks.reshape(planes_total // 2, 2, pair_count, tile_rows, tile_cols)
    rightward = grouped[:, 0]
    leftward = grouped[:, 1]
    from_left = from_behind(rightward[:, :, :, tile_cols - margin :], "sx", 1)
    from_right = from_behind(leftward[:, :, :, :margin], "sx", -1)
    extended_right = jnp.concatenate([from_left, rightward], axis=3)
    extended_left = jnp.concatenate([leftward, from_right], axis=3)
    grouped_offsets = column_offsets.reshape(planes_total // 2, 2)
    moved_right = take_window(extended_right, margin - grouped_offsets[:, 0], tile_cols, 3)
    moved_left = take_window(extended_left, -grouped_offsets[:, 1], tile_cols, 3)
    return jnp.stack([moved_right, moved_left], axis=1).reshape(stacks.shape)


def per_device(
    exposures, psf_kernels, clip_masks, exposure_weights, plane_offsets, start_flux, start_weight
):
    nights_total = exposures.shape[0]
    frames = exposures.shape[1]
    tile_rows = exposures.shape[2]
    kernel_size = psf_kernels.shape[2]
    radius = (kernel_size - 1) // 2
    planes_total = start_flux.shape[0]
    selector = tap_selector(kernel_size, tile_rows)
    powers = 2 ** jnp.arange(planes_total, dtype=jnp.int32)
    stacks = jnp.stack([start_flux, start_weight], axis=1)
    for night_index in range(nights_total):
        if night_index > 0:
            offsets_now = plane_offsets[night_index - 1]
            stacks = shift_columns(shift_rows(stacks, offsets_now[:, 0]), offsets_now[:, 1])

        def exposure_step(frame_index, stacks_now):
            padded = padded_2(exposures[night_index, frame_index], (("sy", 0), ("sx", 1)), radius)
            filtered = filter_tile(padded, psf_kernels[night_index, frame_index], selector)
            return accumulate(
                stacks_now,
                filtered,
                clip_masks[night_index, frame_index],
                exposure_weights[night_index, frame_index],
                powers,
            )

        stacks = lax.fori_loop(0, frames, exposure_step, stacks)
    return (stacks[:, 0], stacks[:, 1])


def solution(mesh):
    return jax.shard_map(
        per_device,
        mesh=mesh,
        in_specs=(
            P(None, None, "sy", "sx"),
            P(),
            P(None, None, "sy", "sx"),
            P(),
            P(),
            P(None, "sy", "sx"),
            P(None, "sy", "sx"),
        ),
        out_specs=(P(None, "sy", "sx"), P(None, "sy", "sx")),
        check_vma=False,
    )
```

profile of v0, /device:TPU:120, one launch (start us, length us, event | category | flops | bytes accessed | tf_op | source)
XLA Modules:
  0.0 1669.7 jit_solution(9577554068001981572)
XLA Ops:
  4.1 339.1 %while.64 = (s32[]{:T(128)}, f32[8,2,64,512]{3,2,1,0:T(8,128)S(1)}, f32[4,8]{1,0:T(4,128)}, s32[4,8,64,512]{3,2,1,0:T(8,128)}, bf16[4,8,21,21]{3,2,1,0:T(8,128)(...) while((s32[]{:T(128)}, f32[8,2,64,512]{3,2,1,0:T(8,128)S(1)}, ...), condition=%wide.region_1.3_spmd.clone, body=%wide.region_0.2_spmd.clone.sunk | while | flops 130176056 | bytes 18905776 | solution.py:131
  35.1 11.5 add_bitcast_fusion.8
  77.4 11.5 add_bitcast_fusion.8
  162.0 11.5 add_bitcast_fusion.8
  204.2 11.5 add_bitcast_fusion.8
  246.5 11.5 add_bitcast_fusion.8
  331.1 11.5 add_bitcast_fusion.8
  443.5 341.2 %while.65 = (s32[]{:T(128)}, f32[8,2,64,512]{3,2,1,0:T(8,128)S(1)}, f32[4,8]{1,0:T(4,128)}, s32[4,8,64,512]{3,2,1,0:T(8,128)}, bf16[4,8,21,21]{3,2,1,0:T(8,128)(...) while((s32[]{:T(128)}, f32[8,2,64,512]{3,2,1,0:T(8,128)S(1)}, ...), condition=%wide.region_3.5_spmd.clone, body=%wide.region_2.4_spmd.clone.sunk | while | flops 130176056 | bytes 18905776 | solution.py:131
  476.8 11.5 add_bitcast_fusion.9
  519.1 11.5 add_bitcast_fusion.9
  561.3 11.5 add_bitcast_fusion.9
  603.6 11.5 add_bitcast_fusion.9
  645.9 11.5 add_bitcast_fusion.9
  688.2 11.5 add_bitcast_fusion.9
  730.4 11.5 add_bitcast_fusion.9
  794.7 12.0 collective-permute-done.20
  885.7 341.0 %while.66 = (s32[]{:T(128)}, f32[8,2,64,512]{3,2,1,0:T(8,128)S(1)}, f32[4,8]{1,0:T(4,128)}, s32[4,8,64,512]{3,2,1,0:T(8,128)}, bf16[4,8,21,21]{3,2,1,0:T(8,128)(...) while((s32[]{:T(128)}, f32[8,2,64,512]{3,2,1,0:T(8,128)S(1)}, ...), condition=%wide.region_5.7_spmd.clone, body=%wide.region_4.6_spmd.clone.sunk | while | flops 130176056 | bytes 18905776 | solution.py:131
  918.6 11.5 add_bitcast_fusion.10
  960.8 11.5 add_bitcast_fusion.10
  1045.4 11.5 add_bitcast_fusion.10
  1087.7 11.5 add_bitcast_fusion.10
  1129.9 11.5 add_bitcast_fusion.10
  1214.5 11.5 add_bitcast_fusion.10
  1236.7 12.0 collective-permute-done.24
  1327.0 340.8 %while.67 = (s32[]{:T(128)}, f32[8,2,64,512]{3,2,1,0:T(8,128)S(1)}, f32[4,8]{1,0:T(4,128)}, s32[4,8,64,512]{3,2,1,0:T(8,128)}, bf16[4,8,21,21]{3,2,1,0:T(8,128)(...) while((s32[]{:T(128)}, f32[8,2,64,512]{3,2,1,0:T(8,128)S(1)}, ...), condition=%wide.region_7.9_spmd.clone, body=%wide.region_6.8_spmd.clone.sunk | while | flops 130176056 | bytes 18905776 | solution.py:131
  1360.1 11.5 add_bitcast_fusion.11
  1402.3 11.5 add_bitcast_fusion.11
  1444.6 11.5 add_bitcast_fusion.11
  1486.9 11.5 add_bitcast_fusion.11
  1529.2 11.5 add_bitcast_fusion.11
  1613.7 11.5 add_bitcast_fusion.11
  1656.0 11.5 add_bitcast_fusion.11
  (2034 shorter events, 1308.0 us)
Async XLA Ops:
  4.8 17.2 %collective-permute-start = (bf16[10,512]{1,0:T(8,128)(2,1)S(1)}, bf16[10,512]{1,0:T(8,128)(2,1)S(1)}, u32[]{:S(2)}, u32[]{:S(2)}) collective-permute-start(bf16[10,512]{1,0:T(8,128)(2,1)S(1)} %get-tuple-element.1198), channel_id=1, source_target_pairs={{16,0},{32,16},{48,32},{64,48},{80,64},{96,80},{112,96},{17,1},{33... | collective-permute-start | bytes 30728 | tf_op jit(solution)/shard_map/while/body/eval_jaxpr/ppermute | solution.py:26
  47.6 17.2 %collective-permute-start = (bf16[10,512]{1,0:T(8,128)(2,1)S(1)}, bf16[10,512]{1,0:T(8,128)(2,1)S(1)}, u32[]{:S(2)}, u32[]{:S(2)}) collective-permute-start(bf16[10,512]{1,0:T(8,128)(2,1)S(1)} %get-tuple-element.1198), channel_id=1, source_target_pairs={{16,0},{32,16},{48,32},{64,48},{80,64},{96,80},{112,96},{17,1},{33... | collective-permute-start | bytes 30728 | tf_op jit(solution)/shard_map/while/body/eval_jaxpr/ppermute | solution.py:26
  89.9 17.2 %collective-permute-start = (bf16[10,512]{1,0:T(8,128)(2,1)S(1)}, bf16[10,512]{1,0:T(8,128)(2,1)S(1)}, u32[]{:S(2)}, u32[]{:S(2)}) collective-permute-start(bf16[10,512]{1,0:T(8,128)(2,1)S(1)} %get-tuple-element.1198), channel_id=1, source_target_pairs={{16,0},{32,16},{48,32},{64,48},{80,64},{96,80},{112,96},{17,1},{33... | collective-permute-start | bytes 30728 | tf_op jit(solution)/shard_map/while/body/eval_jaxpr/ppermute | solution.py:26
  132.2 17.2 %collective-permute-start = (bf16[10,512]{1,0:T(8,128)(2,1)S(1)}, bf16[10,512]{1,0:T(8,128)(2,1)S(1)}, u32[]{:S(2)}, u32[]{:S(2)}) collective-permute-start(bf16[10,512]{1,0:T(8,128)(2,1)S(1)} %get-tuple-element.1198), channel_id=1, source_target_pairs={{16,0},{32,16},{48,32},{64,48},{80,64},{96,80},{112,96},{17,1},{33... | collective-permute-start | bytes 30728 | tf_op jit(solution)/shard_map/while/body/eval_jaxpr/ppermute | solution.py:26
  216.8 17.2 %collective-permute-start = (bf16[10,512]{1,0:T(8,128)(2,1)S(1)}, bf16[10,512]{1,0:T(8,128)(2,1)S(1)}, u32[]{:S(2)}, u32[]{:S(2)}) collective-permute-start(bf16[10,512]{1,0:T(8,128)(2,1)S(1)} %get-tuple-element.1198), channel_id=1, source_target_pairs={{16,0},{32,16},{48,32},{64,48},{80,64},{96,80},{112,96},{17,1},{33... | collective-permute-start | bytes 30728 | tf_op jit(solution)/shard_map/while/body/eval_jaxpr/ppermute | solution.py:26
  301.3 17.2 %collective-permute-start = (bf16[10,512]{1,0:T(8,128)(2,1)S(1)}, bf16[10,512]{1,0:T(8,128)(2,1)S(1)}, u32[]{:S(2)}, u32[]{:S(2)}) collective-permute-start(bf16[10,512]{1,0:T(8,128)(2,1)S(1)} %get-tuple-element.1198), channel_id=1, source_target_pairs={{16,0},{32,16},{48,32},{64,48},{80,64},{96,80},{112,96},{17,1},{33... | collective-permute-start | bytes 30728 | tf_op jit(solution)/shard_map/while/body/eval_jaxpr/ppermute | solution.py:26
  346.3 18.9 %collective-permute-start.16 = (f32[4,2,48,512]{3,1,0,2:T(2,128)S(1)}, f32[4,2,48,512]{3,1,0,2:T(2,128)S(1)}, u32[]{:S(2)}, u32[]{:S(2)}) collective-permute-start(f32[4,2,48,512]{3,1,0,2:T(2,128)S(1)} %get-tuple-element.1023), channel_id=1, source_target_pairs={{0,16},{16,32},{32,48},{48,64},{64,80},{80,96},{96,112},{1,17},{17... | collective-permute-start | bytes 2359304 | tf_op jit(solution)/shard_map/ppermute | solution.py:13
  348.2 22.9 %collective-permute-start.17 = (f32[4,2,48,512]{3,1,0,2:T(2,128)}, f32[4,2,48,512]{3,1,0,2:T(2,128)}, u32[]{:S(2)}, u32[]{:S(2)}) collective-permute-start(f32[4,2,48,512]{3,1,0,2:T(2,128)} %get-tuple-element.1024), channel_id=1, source_target_pairs={{16,0},{32,16},{48,32},{64,48},{80,64},{96,80},{112,96},{17,1},{33... | collective-permute-start | bytes 2359304 | tf_op jit(solution)/shard_map/ppermute | solution.py:13
  444.7 17.2 %collective-permute-start.4 = (bf16[10,512]{1,0:T(8,128)(2,1)S(1)}, bf16[10,512]{1,0:T(8,128)(2,1)S(1)}, u32[]{:S(2)}, u32[]{:S(2)}) collective-permute-start(bf16[10,512]{1,0:T(8,128)(2,1)S(1)} %get-tuple-element.1210), channel_id=1, source_target_pairs={{16,0},{32,16},{48,32},{64,48},{80,64},{96,80},{112,96},{17,1},{33... | collective-permute-start | bytes 30728 | tf_op jit(solution)/shard_map/while/body/eval_jaxpr/ppermute | solution.py:26
  489.3 17.2 %collective-permute-start.4 = (bf16[10,512]{1,0:T(8,128)(2,1)S(1)}, bf16[10,512]{1,0:T(8,128)(2,1)S(1)}, u32[]{:S(2)}, u32[]{:S(2)}) collective-permute-start(bf16[10,512]{1,0:T(8,128)(2,1)S(1)} %get-tuple-element.1210), channel_id=1, source_target_pairs={{16,0},{32,16},{48,32},{64,48},{80,64},{96,80},{112,96},{17,1},{33... | collective-permute-start | bytes 30728 | tf_op jit(solution)/shard_map/while/body/eval_jaxpr/ppermute | solution.py:26
  531.6 17.2 %collective-permute-start.4 = (bf16[10,512]{1,0:T(8,128)(2,1)S(1)}, bf16[10,512]{1,0:T(8,128)(2,1)S(1)}, u32[]{:S(2)}, u32[]{:S(2)}) collective-permute-start(bf16[10,512]{1,0:T(8,128)(2,1)S(1)} %get-tuple-element.1210), channel_id=1, source_target_pairs={{16,0},{32,16},{48,32},{64,48},{80,64},{96,80},{112,96},{17,1},{33... | collective-permute-start | bytes 30728 | tf_op jit(solution)/shard_map/while/body/eval_jaxpr/ppermute | solution.py:26
  573.9 17.2 %collective-permute-start.4 = (bf16[10,512]{1,0:T(8,128)(2,1)S(1)}, bf16[10,512]{1,0:T(8,128)(2,1)S(1)}, u32[]{:S(2)}, u32[]{:S(2)}) collective-permute-start(bf16[10,512]{1,0:T(8,128)(2,1)S(1)} %get-tuple-element.1210), channel_id=1, source_target_pairs={{16,0},{32,16},{48,32},{64,48},{80,64},{96,80},{112,96},{17,1},{33... | collective-permute-start | bytes 30728 | tf_op jit(solution)/shard_map/while/body/eval_jaxpr/ppermute | solution.py:26
  616.1 17.2 %collective-permute-start.4 = (bf16[10,512]{1,0:T(8,128)(2,1)S(1)}, bf16[10,512]{1,0:T(8,128)(2,1)S(1)}, u32[]{:S(2)}, u32[]{:S(2)}) collective-permute-start(bf16[10,512]{1,0:T(8,128)(2,1)S(1)} %get-tuple-element.1210), channel_id=1, source_target_pairs={{16,0},{32,16},{48,32},{64,48},{80,64},{96,80},{112,96},{17,1},{33... | collective-permute-start | bytes 30728 | tf_op jit(solution)/shard_map/while/body/eval_jaxpr/ppermute | solution.py:26
  658.4 17.2 %collective-permute-start.4 = (bf16[10,512]{1,0:T(8,128)(2,1)S(1)}, bf16[10,512]{1,0:T(8,128)(2,1)S(1)}, u32[]{:S(2)}, u32[]{:S(2)}) collective-permute-start(bf16[10,512]{1,0:T(8,128)(2,1)S(1)} %get-tuple-element.1210), channel_id=1, source_target_pairs={{16,0},{32,16},{48,32},{64,48},{80,64},{96,80},{112,96},{17,1},{33... | collective-permute-start | bytes 30728 | tf_op jit(solution)/shard_map/while/body/eval_jaxpr/ppermute | solution.py:26
  700.7 17.2 %collective-permute-start.4 = (bf16[10,512]{1,0:T(8,128)(2,1)S(1)}, bf16[10,512]{1,0:T(8,128)(2,1)S(1)}, u32[]{:S(2)}, u32[]{:S(2)}) collective-permute-start(bf16[10,512]{1,0:T(8,128)(2,1)S(1)} %get-tuple-element.1210), channel_id=1, source_target_pairs={{16,0},{32,16},{48,32},{64,48},{80,64},{96,80},{112,96},{17,1},{33... | collective-permute-start | bytes 30728 | tf_op jit(solution)/shard_map/while/body/eval_jaxpr/ppermute | solution.py:26
  743.0 17.2 %collective-permute-start.4 = (bf16[10,512]{1,0:T(8,128)(2,1)S(1)}, bf16[10,512]{1,0:T(8,128)(2,1)S(1)}, u32[]{:S(2)}, u32[]{:S(2)}) collective-permute-start(bf16[10,512]{1,0:T(8,128)(2,1)S(1)} %get-tuple-element.1210), channel_id=1, source_target_pairs={{16,0},{32,16},{48,32},{64,48},{80,64},{96,80},{112,96},{17,1},{33... | collective-permute-start | bytes 30728 | tf_op jit(solution)/shard_map/while/body/eval_jaxpr/ppermute | solution.py:26
  787.7 18.9 %collective-permute-start.20 = (f32[4,2,48,512]{3,1,0,2:T(2,128)S(1)}, f32[4,2,48,512]{3,1,0,2:T(2,128)S(1)}, u32[]{:S(2)}, u32[]{:S(2)}) collective-permute-start(f32[4,2,48,512]{3,1,0,2:T(2,128)S(1)} %get-tuple-element.1017), channel_id=1, source_target_pairs={{0,16},{16,32},{32,48},{48,64},{64,80},{80,96},{96,112},{1,17},{17... | collective-permute-start | bytes 2359304 | tf_op jit(solution)/shard_map/ppermute | solution.py:13
  789.7 22.9 %collective-permute-start.21 = (f32[4,2,48,512]{3,1,0,2:T(2,128)}, f32[4,2,48,512]{3,1,0,2:T(2,128)}, u32[]{:S(2)}, u32[]{:S(2)}) collective-permute-start(f32[4,2,48,512]{3,1,0,2:T(2,128)} %get-tuple-element.1018), channel_id=1, source_target_pairs={{16,0},{32,16},{48,32},{64,48},{80,64},{96,80},{112,96},{17,1},{33... | collective-permute-start | bytes 2359304 | tf_op jit(solution)/shard_map/ppermute | solution.py:13
  886.6 17.2 %collective-permute-start.8 = (bf16[10,512]{1,0:T(8,128)(2,1)S(1)}, bf16[10,512]{1,0:T(8,128)(2,1)S(1)}, u32[]{:S(2)}, u32[]{:S(2)}) collective-permute-start(bf16[10,512]{1,0:T(8,128)(2,1)S(1)} %get-tuple-element.1222), channel_id=1, source_target_pairs={{16,0},{32,16},{48,32},{64,48},{80,64},{96,80},{112,96},{17,1},{33... | collective-permute-start | bytes 30728 | tf_op jit(solution)/shard_map/while/body/eval_jaxpr/ppermute | solution.py:26
  931.1 17.2 %collective-permute-start.8 = (bf16[10,512]{1,0:T(8,128)(2,1)S(1)}, bf16[10,512]{1,0:T(8,128)(2,1)S(1)}, u32[]{:S(2)}, u32[]{:S(2)}) collective-permute-start(bf16[10,512]{1,0:T(8,128)(2,1)S(1)} %get-tuple-element.1222), channel_id=1, source_target_pairs={{16,0},{32,16},{48,32},{64,48},{80,64},{96,80},{112,96},{17,1},{33... | collective-permute-start | bytes 30728 | tf_op jit(solution)/shard_map/while/body/eval_jaxpr/ppermute | solution.py:26
  973.4 17.2 %collective-permute-start.8 = (bf16[10,512]{1,0:T(8,128)(2,1)S(1)}, bf16[10,512]{1,0:T(8,128)(2,1)S(1)}, u32[]{:S(2)}, u32[]{:S(2)}) collective-permute-start(bf16[10,512]{1,0:T(8,128)(2,1)S(1)} %get-tuple-element.1222), channel_id=1, source_target_pairs={{16,0},{32,16},{48,32},{64,48},{80,64},{96,80},{112,96},{17,1},{33... | collective-permute-start | bytes 30728 | tf_op jit(solution)/shard_map/while/body/eval_jaxpr/ppermute | solution.py:26
  1057.9 17.2 %collective-permute-start.8 = (bf16[10,512]{1,0:T(8,128)(2,1)S(1)}, bf16[10,512]{1,0:T(8,128)(2,1)S(1)}, u32[]{:S(2)}, u32[]{:S(2)}) collective-permute-start(bf16[10,512]{1,0:T(8,128)(2,1)S(1)} %get-tuple-element.1222), channel_id=1, source_target_pairs={{16,0},{32,16},{48,32},{64,48},{80,64},{96,80},{112,96},{17,1},{33... | collective-permute-start | bytes 30728 | tf_op jit(solution)/shard_map/while/body/eval_jaxpr/ppermute | solution.py:26
  1100.2 17.2 %collective-permute-start.8 = (bf16[10,512]{1,0:T(8,128)(2,1)S(1)}, bf16[10,512]{1,0:T(8,128)(2,1)S(1)}, u32[]{:S(2)}, u32[]{:S(2)}) collective-permute-start(bf16[10,512]{1,0:T(8,128)(2,1)S(1)} %get-tuple-element.1222), channel_id=1, source_target_pairs={{16,0},{32,16},{48,32},{64,48},{80,64},{96,80},{112,96},{17,1},{33... | collective-permute-start | bytes 30728 | tf_op jit(solution)/shard_map/while/body/eval_jaxpr/ppermute | solution.py:26
  1184.8 17.2 %collective-permute-start.8 = (bf16[10,512]{1,0:T(8,128)(2,1)S(1)}, bf16[10,512]{1,0:T(8,128)(2,1)S(1)}, u32[]{:S(2)}, u32[]{:S(2)}) collective-permute-start(bf16[10,512]{1,0:T(8,128)(2,1)S(1)} %get-tuple-element.1222), channel_id=1, source_target_pairs={{16,0},{32,16},{48,32},{64,48},{80,64},{96,80},{112,96},{17,1},{33... | collective-permute-start | bytes 30728 | tf_op jit(solution)/shard_map/while/body/eval_jaxpr/ppermute | solution.py:26
  1229.7 18.9 %collective-permute-start.24 = (f32[4,2,48,512]{3,1,0,2:T(2,128)S(1)}, f32[4,2,48,512]{3,1,0,2:T(2,128)S(1)}, u32[]{:S(2)}, u32[]{:S(2)}) collective-permute-start(f32[4,2,48,512]{3,1,0,2:T(2,128)S(1)} %get-tuple-element.1011), channel_id=1, source_target_pairs={{0,16},{16,32},{32,48},{48,64},{64,80},{80,96},{96,112},{1,17},{17... | collective-permute-start | bytes 2359304 | tf_op jit(solution)/shard_map/ppermute | solution.py:13
  1231.7 22.9 %collective-permute-start.25 = (f32[4,2,48,512]{3,1,0,2:T(2,128)}, f32[4,2,48,512]{3,1,0,2:T(2,128)}, u32[]{:S(2)}, u32[]{:S(2)}) collective-permute-start(f32[4,2,48,512]{3,1,0,2:T(2,128)} %get-tuple-element.1012), channel_id=1, source_target_pairs={{16,0},{32,16},{48,32},{64,48},{80,64},{96,80},{112,96},{17,1},{33... | collective-permute-start | bytes 2359304 | tf_op jit(solution)/shard_map/ppermute | solution.py:13
  1328.0 17.2 %collective-permute-start.12 = (bf16[10,512]{1,0:T(8,128)(2,1)S(1)}, bf16[10,512]{1,0:T(8,128)(2,1)S(1)}, u32[]{:S(2)}, u32[]{:S(2)}) collective-permute-start(bf16[10,512]{1,0:T(8,128)(2,1)S(1)} %get-tuple-element.1234), channel_id=1, source_target_pairs={{16,0},{32,16},{48,32},{64,48},{80,64},{96,80},{112,96},{17,1},{33... | collective-permute-start | bytes 30728 | tf_op jit(solution)/shard_map/while/body/eval_jaxpr/ppermute | solution.py:26
  1372.6 17.2 %collective-permute-start.12 = (bf16[10,512]{1,0:T(8,128)(2,1)S(1)}, bf16[10,512]{1,0:T(8,128)(2,1)S(1)}, u32[]{:S(2)}, u32[]{:S(2)}) collective-permute-start(bf16[10,512]{1,0:T(8,128)(2,1)S(1)} %get-tuple-element.1234), channel_id=1, source_target_pairs={{16,0},{32,16},{48,32},{64,48},{80,64},{96,80},{112,96},{17,1},{33... | collective-permute-start | bytes 30728 | tf_op jit(solution)/shard_map/while/body/eval_jaxpr/ppermute | solution.py:26
  1414.9 17.2 %collective-permute-start.12 = (bf16[10,512]{1,0:T(8,128)(2,1)S(1)}, bf16[10,512]{1,0:T(8,128)(2,1)S(1)}, u32[]{:S(2)}, u32[]{:S(2)}) collective-permute-start(bf16[10,512]{1,0:T(8,128)(2,1)S(1)} %get-tuple-element.1234), channel_id=1, source_target_pairs={{16,0},{32,16},{48,32},{64,48},{80,64},{96,80},{112,96},{17,1},{33... | collective-permute-start | bytes 30728 | tf_op jit(solution)/shard_map/while/body/eval_jaxpr/ppermute | solution.py:26
  1499.4 17.2 %collective-permute-start.12 = (bf16[10,512]{1,0:T(8,128)(2,1)S(1)}, bf16[10,512]{1,0:T(8,128)(2,1)S(1)}, u32[]{:S(2)}, u32[]{:S(2)}) collective-permute-start(bf16[10,512]{1,0:T(8,128)(2,1)S(1)} %get-tuple-element.1234), channel_id=1, source_target_pairs={{16,0},{32,16},{48,32},{64,48},{80,64},{96,80},{112,96},{17,1},{33... | collective-permute-start | bytes 30728 | tf_op jit(solution)/shard_map/while/body/eval_jaxpr/ppermute | solution.py:26
  1541.7 17.2 %collective-permute-start.12 = (bf16[10,512]{1,0:T(8,128)(2,1)S(1)}, bf16[10,512]{1,0:T(8,128)(2,1)S(1)}, u32[]{:S(2)}, u32[]{:S(2)}) collective-permute-start(bf16[10,512]{1,0:T(8,128)(2,1)S(1)} %get-tuple-element.1234), channel_id=1, source_target_pairs={{16,0},{32,16},{48,32},{64,48},{80,64},{96,80},{112,96},{17,1},{33... | collective-permute-start | bytes 30728 | tf_op jit(solution)/shard_map/while/body/eval_jaxpr/ppermute | solution.py:26
  1626.2 17.2 %collective-permute-start.12 = (bf16[10,512]{1,0:T(8,128)(2,1)S(1)}, bf16[10,512]{1,0:T(8,128)(2,1)S(1)}, u32[]{:S(2)}, u32[]{:S(2)}) collective-permute-start(bf16[10,512]{1,0:T(8,128)(2,1)S(1)} %get-tuple-element.1234), channel_id=1, source_target_pairs={{16,0},{32,16},{48,32},{64,48},{80,64},{96,80},{112,96},{17,1},{33... | collective-permute-start | bytes 30728 | tf_op jit(solution)/shard_map/while/body/eval_jaxpr/ppermute | solution.py:26
  (375 other events, 1831.9 us)
where the time goes:
time: 1690 us; the launch traced here: 1670 us
  other arithmetic  586 us (35%)
  starting transfers between devices  483 us (29%)
  local copies, waits for them, and re-layouts  384 us (23%)
  waiting for transfers between devices  130 us (8%)
  matrix products  47.8 us (3%)
  loops' own time  36.8 us (2%)
    another operation x64, other arithmetic, accumulate(): jnp.stack([flux_stack + weight_value * chosen, weight_stack + weight_valu...  376 us
    ppermute x64, starting transfers between devices, padded_2(): lax.ppermute(tail, axis, [(i, (i + 1) % count) for i in range(ends)])  316 us
    ppermute x64, starting transfers between devices, padded_2(): lax.ppermute(head, axis, [((i + 1) % count, i) for i in range(ends)])  130 us
    ppermute x64, waiting for transfers between devices, padded_2(): lax.ppermute(tail, axis, [(i, (i + 1) % count) for i in range(ends)])  86.1 us
    ne x64, other arithmetic, accumulate(): clip_bits = clip_mask[None] // powers[:, None, None] % 2  67.4 us
    while x1120, local copies, waits for them, and re-layouts  54.2 us
    gather x12, local copies, waits for them, and re-layouts, window_one(): return lax.dynamic_slice_in_dim(single, first_cell, length, axis_number - 1)  52 us
    rem x32, local copies, waits for them, and re-layouts, accumulate(): clip_bits = clip_mask[None] // powers[:, None, None] % 2  50.9 us
  transfers between devices with their start and end apart: 140, of which 41 were waited for; matrix products, arithmetic and copies ran while one was open for 20% of the time, Pallas kernels for 0%

commit v1 on v0

v1 whole, which is shorter than its diff:
```python
import jax
import jax.numpy as jnp
from jax import lax
from jax.experimental import pallas as pl
from jax.experimental.pallas import tpu as pltpu
from jax.sharding import PartitionSpec as P

f32, bf16, i32 = jnp.float32, jnp.bfloat16, jnp.int32
band_scale = 1.5
weight_floor = 1.0
ROWS, COLS = 64, 512
MR, MC = 48, 384
PLANES, NIGHTS, EXPS, KS, RAD = 8, 4, 8, 21, 10
NEXP = NIGHTS * EXPS
STEP = 16


def send(value, axis, steps):
    count = lax.axis_size(axis)
    first, last = max(0, -steps), min(count, count - steps)
    return lax.ppermute(value, axis, [(s, s + steps) for s in range(first, last)])


def conv_body(z, kv, wbuf, zwin):
    for b in range(KS):
        b0, ph = b // 4, b % 4
        base = jnp.broadcast_to(kv[b : b + 1, :], (ROWS, 128))
        t = pltpu.roll(base, 0, 1, stride=1, stride_axis=0)
        wbuf[ph * 64 : (ph + 1) * 64, b0 * 128 : (b0 + 1) * 128] = t.astype(bf16)
    for b0 in range(6):
        zwin[b0 * 128 : (b0 + 1) * 128, :] = pltpu.roll(z, (RAD - 4 * b0) % 640, 1)
    acc = jnp.dot(wbuf[...], zwin[...], preferred_element_type=f32)
    out = acc[0:64, 0:COLS]
    for ph in range(1, 4):
        out = out + pltpu.roll(acc[ph * 64 : (ph + 1) * 64, :], 640 - ph, 1)[:, :COLS]
    return out


def conv_kernel(z_ref, kv_ref, o_ref, wbuf, zwin):
    @pl.when(pl.program_id(0) == 0)
    def _():
        wbuf[...] = jnp.zeros_like(wbuf)

    o_ref[0] = conv_body(z_ref[0], kv_ref[0], wbuf, zwin)


def conv_call(z, kv):
    return pl.pallas_call(
        conv_kernel,
        grid=(NEXP,),
        in_specs=[
            pl.BlockSpec((1, 128, 640), lambda i: (i, 0, 0)),
            pl.BlockSpec((1, 24, 128), lambda i: (i, 0, 0)),
        ],
        out_specs=pl.BlockSpec((1, ROWS, COLS), lambda i: (i, 0, 0)),
        out_shape=jax.ShapeDtypeStruct((NEXP, ROWS, COLS), f32),
        scratch_shapes=[pltpu.VMEM((256, 768), bf16), pltpu.VMEM((768, 640), bf16)],
        name="conv",
    )(z, kv)


def update_rows(flux, weight, filt_ref, mask_ref, rows, bit, wv_ref, night):
    for e in range(EXPS):
        wv = wv_ref[night, e]
        half = wv_ref[night, EXPS + e]
        filtered = filt_ref[e, rows, :]
        mask = mask_ref[e, rows, :]
        mean = flux / jnp.maximum(weight, weight_floor)
        clipped = jnp.clip(filtered, mean - half, mean + half)
        chosen = jnp.where((mask & bit) != 0, clipped, filtered)
        flux = flux + wv * chosen
        weight = weight + wv
    return flux, weight


def pack_plane(fbuf, wbuf, peak, enc, own, exps):
    for k in (4, 2, 1):
        peak = jnp.maximum(peak, pltpu.roll(peak, k, 0))
    expo = jnp.ceil(4.0 * jnp.log2(jnp.maximum(peak, 1e-30)) + 0.01)
    gain = jnp.exp2(expo * -0.25) * 32766.0
    exps[...] = expo.astype(i32)

    def step(i, c):
        rows = pl.ds(pl.multiple_of(i * 8, 8), 8)
        q = jnp.round(fbuf[rows, :] * gain).astype(i32)
        w = (wbuf[rows, :] * enc + 0.5).astype(i32)
        own[rows, :] = (q << 16) | w
        return c

    lax.fori_loop(0, ROWS // 8, step, 0)


def night_kernel(night, *refs):
    refs = list(refs)
    wv_ref = refs.pop(0)
    off_ref = refs.pop(0)
    first, final = night == 0, night == NIGHTS - 1
    if first:
        flux_ref, weight_ref = refs.pop(0), refs.pop(0)
    else:
        s_ref, r_ref = refs.pop(0), refs.pop(0)
    filt_ref, mask_ref = refs.pop(0), refs.pop(0)
    if final:
        oflux, oweight = refs.pop(0), refs.pop(0)
    else:
        own, exps = refs.pop(0), refs.pop(0)
        fbuf, wbuf = refs.pop(0), refs.pop(0)
    p = pl.program_id(0)
    bit = jnp.left_shift(jnp.int32(1), p)
    if not first:
        cext = refs.pop(0)

        @pl.when(p % 2 == 0)
        def _():
            cext[:, :MC] = r_ref[0]
            cext[:, MC : MC + COLS] = s_ref[0]

        @pl.when(p % 2 == 1)
        def _():
            cext[:, :COLS] = s_ref[0]
            cext[:, COLS : COLS + MC] = r_ref[0]

        row_off = off_ref[night - 1, 2 * p]
        col_off = off_ref[night - 1, 2 * p + 1]
        start = jnp.where(p % 2 == 0, MC - col_off, -col_off)
        tile = pl.multiple_of((start // 128) * 128, 128)
        turn = (640 - start % 128) % 640

        def window(rows):
            return pltpu.roll(cext[rows, pl.ds(tile, 640)], turn, 1)[:, :COLS]

        own_gain = jnp.exp2(window(pl.ds(64, 8)).astype(f32) * 0.25) * (1.0 / 32766.0)
        far_gain = jnp.exp2(window(pl.ds(72, 8)).astype(f32) * 0.25) * (1.0 / 32766.0)
        own_gain = jnp.concatenate([own_gain, own_gain], axis=0)
        far_gain = jnp.concatenate([far_gain, far_gain], axis=0)
        dec = wv_ref[night, 2 * EXPS]
        lo = jnp.where(p < 4, row_off, 0)
        hi = jnp.where(p < 4, ROWS, ROWS + row_off)
        lane_row = lax.broadcasted_iota(i32, (STEP, COLS), 0)

    def step(i, peak):
        rows = pl.ds(pl.multiple_of(i * STEP, STEP), STEP)
        if first:
            flux, weight = flux_ref[0, rows, :], weight_ref[0, rows, :]
        else:
            packed = window(rows)
            y = lane_row + i * STEP
            gain = jnp.where((y >= lo) & (y < hi), own_gain, far_gain)
            flux = (packed >> 16).astype(f32) * gain
            weight = (packed & 0xFFFF).astype(f32) * dec
        flux, weight = update_rows(flux, weight, filt_ref, mask_ref, rows, bit, wv_ref, night)
        if final:
            oflux[0, rows, :] = flux
            oweight[0, rows, :] = weight
            return peak
        fbuf[rows, :] = flux
        wbuf[rows, :] = weight
        size = jnp.abs(flux)
        return jnp.maximum(peak, jnp.maximum(size[:8], size[8:]))

    peak = lax.fori_loop(0, ROWS // STEP, step, jnp.zeros((8, COLS), f32))
    if not final:
        pack_plane(fbuf, wbuf, peak, wv_ref[night, 2 * EXPS + 1], own.at[0], exps.at[0])


def night_call(night, table, offsets, state, filt, masks):
    first, final = night == 0, night == NIGHTS - 1
    plane = lambda rows, cols: pl.BlockSpec((1, rows, cols), lambda p: (p, 0, 0))
    whole = pl.BlockSpec((EXPS, ROWS, COLS), lambda p: (night, 0, 0))
    state_specs = [plane(ROWS, COLS)] * 2 if first else [plane(80, COLS), plane(80, MC)]
    if final:
        out_specs = [plane(ROWS, COLS)] * 2
        out_shape = [jax.ShapeDtypeStruct((PLANES, ROWS, COLS), f32)] * 2
        scratch = []
    else:
        out_specs = [plane(ROWS, COLS), plane(8, COLS)]
        out_shape = [
            jax.ShapeDtypeStruct((PLANES, ROWS, COLS), i32),
            jax.ShapeDtypeStruct((PLANES, 8, COLS), i32),
        ]
        scratch = [pltpu.VMEM((ROWS, COLS), f32)] * 2
    if not first:
        scratch = scratch + [pltpu.VMEM((80, 1024), i32)]
    smem = pl.BlockSpec(memory_space=pltpu.SMEM)
    return pl.pallas_call(
        lambda *refs: night_kernel(night, *refs),
        grid=(PLANES,),
        in_specs=[smem, smem] + state_specs + [whole, whole],
        out_specs=out_specs,
        out_shape=out_shape,
        scratch_shapes=scratch,
        name=f"night{night}",
    )(table, offsets, *state, filt, masks)


def row_kernel(night, off_ref, own, exps, recv, out, ext):
    p = pl.program_id(0)
    row_off = off_ref[night - 1, 2 * p]

    @pl.when(p < 4)
    def _():
        ext[:MR, :] = recv[0, :MR, :]
        ext[MR : MR + ROWS, :] = own[0]

    @pl.when(p >= 4)
    def _():
        ext[:ROWS, :] = own[0]
        ext[ROWS : ROWS + MR, :] = recv[0, :MR, :]

    start = jnp.where(p < 4, MR - row_off, -row_off)
    base = pl.multiple_of((start // 8) * 8, 8)
    out[0, :ROWS, :] = pltpu.roll(ext[pl.ds(base, ROWS + 8), :], (72 - start % 8) % 72, 0)[:ROWS]
    out[0, ROWS : ROWS + 8, :] = exps[0]
    out[0, ROWS + 8 :, :] = recv[0, MR:, :]


def row_call(night, offsets, own, exps, recv):
    plane = lambda rows: pl.BlockSpec((1, rows, COLS), lambda p: (p, 0, 0))
    return pl.pallas_call(
        lambda *refs: row_kernel(night, *refs),
        grid=(PLANES,),
        in_specs=[pl.BlockSpec(memory_space=pltpu.SMEM), plane(ROWS), plane(8), plane(MR + 8)],
        out_specs=plane(80),
        out_shape=jax.ShapeDtypeStruct((PLANES, 80, COLS), i32),
        scratch_shapes=[pltpu.VMEM((ROWS + MR + 8, COLS), i32)],
        name=f"rows{night}",
    )(offsets, own, exps, recv)


def scalar_table(exposure_weights):
    totals = 4.0 + jnp.cumsum(jnp.sum(exposure_weights, axis=1))
    top = totals * 1.0001
    enc = 65535.0 / top
    dec = jnp.concatenate([jnp.ones((1,), f32), top[:-1] / 65535.0])
    half = band_scale / jnp.sqrt(exposure_weights)
    return jnp.concatenate([exposure_weights, half, dec[:, None], enc[:, None]], axis=1)


def kernel_rows(psf_kernels):
    k = psf_kernels.astype(f32).reshape(NEXP, KS, KS).transpose(0, 2, 1)
    gap = jnp.zeros((NEXP, KS, 128 - KS), f32)
    k = jnp.concatenate([k[:, :, RAD:], gap, k[:, :, :RAD]], axis=2)
    return jnp.pad(k, ((0, 0), (0, 3), (0, 0)))


def per_device(exposures, psf_kernels, clip_masks, exposure_weights, plane_offsets, flux, weight):
    e = exposures.reshape(NEXP, ROWS, COLS)
    masks = clip_masks.reshape(NEXP, ROWS, COLS)
    table = scalar_table(exposure_weights)
    offsets = plane_offsets.reshape(NIGHTS - 1, 2 * PLANES)
    above = send(e[:, ROWS - RAD :, :], "sy", 1)
    below = send(e[:, :RAD, :], "sy", -1)
    tall = jnp.concatenate([e, below, jnp.zeros((NEXP, 44, COLS), bf16), above], axis=1)
    left = send(tall[:, :, COLS - RAD :], "sx", 1)
    right = send(tall[:, :, :RAD], "sx", -1)
    z = jnp.concatenate([tall, right, jnp.zeros((NEXP, 128, 108), bf16), left], axis=2)
    filt = conv_call(z, kernel_rows(psf_kernels))
    state = (flux, weight)
    for night in range(NIGHTS):
        if night > 0:
            own, exps = state
            down = jnp.concatenate([own[:4, ROWS - MR :, :], exps[:4]], axis=1)
            up = jnp.concatenate([own[4:, :MR, :], exps[4:]], axis=1)
            recv = jnp.concatenate([send(down, "sy", 1), send(up, "sy", -1)], axis=0)
            moved = row_call(night, offsets, own, exps, recv)
            pairs = moved.reshape(4, 2, 80, COLS)
            r = send(pairs[:, 0, :, COLS - MC :], "sx", 1)
            l = send(pairs[:, 1, :, :MC], "sx", -1)
            state = (moved, jnp.stack([r, l], axis=1).reshape(PLANES, 80, MC))
        state = night_call(night, table, offsets, state, filt, masks)
    return tuple(state)


def solution(mesh):
    return jax.shard_map(
        per_device,
        mesh=mesh,
        in_specs=(
            P(None, None, "sy", "sx"),
            P(),
            P(None, None, "sy", "sx"),
            P(),
            P(),
            P(None, "sy", "sx"),
            P(None, "sy", "sx"),
        ),
        out_specs=(P(None, "sy", "sx"), P(None, "sy", "sx")),
        check_vma=False,
    )
```

time: 1690 us -> 265 us (0.16)
  the two profiles are of different devices: /device:TPU:120 before, /device:TPU:97 now
where the time goes in v1:
time: 265 us; the launch traced here: 262 us
  Pallas kernels  90.3 us (34%)
  waiting for transfers between devices  73.6 us (28%)
  starting transfers between devices  61.8 us (23%)
  local copies, waits for them, and re-layouts  17.9 us (7%)
  other arithmetic  17.5 us (7%)
    ppermute x16, waiting for transfers between devices, send(): lax.ppermute(value, axis, [(s, s + steps) for s in range(first, last)])  73.6 us
    ppermute x16, starting transfers between devices, send(): lax.ppermute(value, axis, [(s, s + steps) for s in range(first, last)])  61.8 us
    pallas_call x4, Pallas kernels, night_call(): pl.pallas_call(lambda *refs: night_kernel(night, *refs), grid=(PLANES,),...  42.7 us
    pallas_call x1, Pallas kernels, conv_call(): pl.pallas_call(conv_kernel, grid=(NEXP,), in_specs=[pl.BlockSpec((1, 128,...  30.1 us
    pallas_call x3, Pallas kernels, row_call(): pl.pallas_call(lambda *refs: row_kernel(night, *refs), grid=(PLANES,), in...  17.5 us
    concatenate x1, other arithmetic, per_device(): jnp.concatenate([tall, right, jnp.zeros((NEXP, 128, 108), bf16), left], a...  6.97 us
    slice x6, local copies, waits for them, and re-layouts, per_device(): down = jnp.concatenate([own[:4, ROWS - MR:, :], exps[:4]], axis=1)  6.22 us
  transfers between devices with their start and end apart: 16, of which 14 were waited for; matrix products, arithmetic and copies ran while one was open for 2% of the time, Pallas kernels for 0%

profile of v1, /device:TPU:97, one launch (start us, length us, event | category | flops | bytes accessed | tf_op | source)
XLA Modules:
  0.0 262.0 jit_solution(5969580815411477312)
XLA Ops:
  4.1 6.9 %collective-permute-start.1 = (bf16[32,10,512]{2,1,0:T(8,128)(2,1)S(1)}, bf16[32,10,512]{2,1,0:T(8,128)(2,1)}, u32[]{:S(2)}, u32[]{:S(2)}) collective-permute-start(bf16[32,10,512]{2,1,0:T(8,128)(2,1)S(1)} %get-tuple-element.17), channel_id=1, source_target_pairs={{0,16},{16,32},{32,48},{48,64},{64,80},{80,96},{96,112},{1,17},{17... | collective-permute-start | bytes 983048 | tf_op jit(solution)/shard_map/ppermute | solution.py:21
  13.9 6.5 %collective-permute-done = bf16[32,10,512]{2,1,0:T(8,128)(2,1)S(1)} collective-permute-done((bf16[32,10,512]{2,1,0:T(8,128)(2,1)S(1)}, bf16[32,10,512]{2,1,0:T(8,128)(2,1)S(1)}, u32[]{:S(2)}, u32[]{:S(2)}) %collective-permute-start) | collective-permute-done | bytes 327712 | tf_op jit(solution)/shard_map/ppermute | solution.py:21
  21.5 3.1 %pad_maximum_fusion.4 = (bf16[32,128,10]{2,1,0:T(8,128)(2,1)}, bf16[32,128,10]{2,1,0:T(8,128)(2,1)S(1)}) fusion(bf16[32,10,512]{2,1,0:T(8,128)(2,1)} %collective-permute-done.1, bf16[32,44,512]{2,1,0:T(8,128)(2,1)S(1)} %broadcast_in_dim.14, bf16[32,10,512]{2,1,0:T(8,128)(2,1)S(1)} %collective-permute-done, bf16[32,64,512]{2,1,0:T(8,128)(2,1)} %bitcast.50), kind=kLoop, calls=%fused_computation.4 | loop fusion | flops 655360 | bytes 4358144 | tf_op jit(solution)/shard_map/slice | solution.py:255
  26.2 3.7 %collective-permute-start.2 = (bf16[32,128,10]{1,0,2:T(8,128)(2,1)S(1)}, bf16[32,128,10]{1,0,2:T(8,128)(2,1)S(1)}, u32[]{:S(2)}, u32[]{:S(2)}) collective-permute-start(bf16[32,128,10]{1,0,2:T(8,128)(2,1)S(1)} %copy.32), channel_id=1, source_target_pairs={{1,0},{2,1},{3,2},{4,3},{5,4},{6,5},{7,6},{8,7},{9,8},{10,9},{11,1... | collective-permute-start | bytes 245768 | tf_op jit(solution)/shard_map/ppermute | solution.py:21
  30.4 3.0 %collective-permute-start.3 = (bf16[32,128,10]{1,0,2:T(8,128)(2,1)S(1)}, bf16[32,128,10]{1,0,2:T(8,128)(2,1)S(1)}, u32[]{:S(2)}, u32[]{:S(2)}) collective-permute-start(bf16[32,128,10]{1,0,2:T(8,128)(2,1)S(1)} %copy.33), channel_id=1, source_target_pairs={{0,1},{1,2},{2,3},{3,4},{4,5},{5,6},{6,7},{7,8},{8,9},{9,10},{10,1... | collective-permute-start | bytes 245768 | tf_op jit(solution)/shard_map/ppermute | solution.py:21
  36.2 7.0 %pad_maximum_fusion.z_ref = bf16[32,128,640]{2,1,0:T(8,128)(2,1)} fusion(bf16[32,128,10]{2,1,0:T(8,128)(2,1)} %copy.35, bf16[32,128,10]{2,1,0:T(8,128)(2,1)S(1)} %copy.34, bf16[32,10,512]{2,1,0:T(8,128)(2,1)} %collective-permute-done.1, bf16[32,44,512]{2,1,0:T(8,128)(2,1)S(1)} %broadcast_in_dim.14, bf16[32,10,512]{2,1,0:T(8,128)(2,1)S(1)} %collective-permute-done, ...), kind=kLoop, calls=%fused_computation | loop fusion | flops 36700160 | bytes 9602304 | tf_op jit(solution)/shard_map/concatenate | solution.py:256
  43.2 30.1 %conv.1.refs_4_ = f32[32,64,512]{2,1,0:T(8,128)} custom-call(bf16[32,128,640]{2,1,0:T(8,128)(2,1)} %pad_maximum_fusion.z_ref, f32[32,24,128]{2,1,0:T(8,128)} %pad.4.kv_ref), custom_call_target="tpu_custom_call" | custom-call | tf_op jit(solution)/shard_map/conv/pallas_call | solution.py:48
  73.3 8.6 %night0.1 = (s32[8,64,512]{2,1,0:T(8,128)}, s32[8,8,512]{2,1,0:T(8,128)}) custom-call(f32[4,18]{1,0:T(4,128)} %pad_maximum_fusion.6.refs_0_, s32[3,16]{1,0:T(4,128)} %reshape.59.refs_1_.refs_0_, f32[8,64,512]{2,1,0:T(8,128)} %refs_2_.1, f32[8,64,512]{2,1,0:T(8,128)} %refs_3_.1, f32[32,64,512]{2,1,0:T(8,128)} %conv.1.refs_4_, s32[32,64,512]{2,1,0:T(8,128)} %bitcast.45), custom_call_target="tpu_custom_call" | custom-call | tf_op jit(solution)/shard_map/night0/pallas_call | solution.py:185
  84.0 8.4 %collective-permute-start.4 = (s32[4,56,512]{2,1,0:T(8,128)S(1)}, s32[4,56,512]{2,1,0:T(8,128)S(1)}, u32[]{:S(2)}, u32[]{:S(2)}) collective-permute-start(s32[4,56,512]{2,1,0:T(8,128)S(1)} %pad_add_fusion.6), channel_id=1, source_target_pairs={{0,16},{16,32},{32,48},{48,64},{64,80},{80,96},{96,112},{1,17},{17... | collective-permute-start | bytes 1376264 | tf_op jit(solution)/shard_map/ppermute | solution.py:21
  94.4 7.3 %collective-permute-done.4 = s32[4,56,512]{2,1,0:T(8,128)S(1)} collective-permute-done((s32[4,56,512]{2,1,0:T(8,128)S(1)}, s32[4,56,512]{2,1,0:T(8,128)S(1)}, u32[]{:S(2)}, u32[]{:S(2)}) %collective-permute-start.4) | collective-permute-done | bytes 458784 | tf_op jit(solution)/shard_map/ppermute | solution.py:21
  101.7 7.8 %collective-permute-done.5 = s32[4,56,512]{2,1,0:T(8,128)S(1)} collective-permute-done((s32[4,56,512]{2,1,0:T(8,128)S(1)}, s32[4,56,512]{2,1,0:T(8,128)S(1)}, u32[]{:S(2)}, u32[]{:S(2)}) %collective-permute-start.5) | collective-permute-done | bytes 458784 | tf_op jit(solution)/shard_map/ppermute | solution.py:21
  110.5 5.8 %rows1.1.refs_2_ = s32[8,80,512]{2,1,0:T(8,128)} custom-call(s32[3,16]{1,0:T(4,128)} %reshape.59.refs_1_.refs_0_, s32[8,64,512]{2,1,0:T(8,128)} %get-tuple-element.8.refs_1_, s32[8,8,512]{2,1,0:T(8,128)} %get-tuple-element.9.refs_2_, s32[8,56,512]{2,1,0:T(8,128)} %pad_add_fusion.3.refs_3_), custom_call_target="tpu_custom_call" | custom-call | tf_op jit(solution)/shard_map/rows1/pallas_call | solution.py:219
  119.5 3.6 %collective-permute-start.6 = (s32[4,80,384]{2,1,0:T(8,128)S(1)}, s32[4,80,384]{2,1,0:T(8,128)S(1)}, u32[]{:S(2)}, u32[]{:S(2)}) collective-permute-start(s32[4,80,384]{2,1,0:T(8,128)S(1)} %get-tuple-element.22), channel_id=1, source_target_pairs={{0,1},{1,2},{2,3},{3,4},{4,5},{5,6},{6,7},{7,8},{8,9},{9,10},{10,1... | collective-permute-start | bytes 1474568 | tf_op jit(solution)/shard_map/ppermute | solution.py:21
  123.1 6.2 %collective-permute-done.7 = s32[4,80,384]{2,1,0:T(8,128)S(1)} collective-permute-done((s32[4,80,384]{2,1,0:T(8,128)S(1)}, s32[4,80,384]{2,1,0:T(8,128)S(1)}, u32[]{:S(2)}, u32[]{:S(2)}) %collective-permute-start.7) | collective-permute-done | bytes 491552 | tf_op jit(solution)/shard_map/ppermute | solution.py:21
  130.3 11.7 %night1.1 = (s32[8,64,512]{2,1,0:T(8,128)}, s32[8,8,512]{2,1,0:T(8,128)}) custom-call(f32[4,18]{1,0:T(4,128)} %pad_maximum_fusion.6.refs_0_, s32[3,16]{1,0:T(4,128)} %reshape.59.refs_1_.refs_0_, s32[8,80,512]{2,1,0:T(8,128)} %rows1.1.refs_2_, s32[8,80,384]{2,1,0:T(8,128)} %bitcast.56, f32[32,64,512]{2,1,0:T(8,128)} %conv.1.refs_4_, s32[32,64,512]{2,1,0:T(8,128)} %bitcast.46), custom_call_target="tpu_custom_call" | custom-call | tf_op jit(solution)/shard_map/night1/pallas_call | solution.py:185
  144.2 2.2 collective-permute-start.8
  146.4 3.1 %collective-permute-start.9 = (s32[4,56,512]{2,1,0:T(8,128)S(1)}, s32[4,56,512]{2,1,0:T(8,128)S(1)}, u32[]{:S(2)}, u32[]{:S(2)}) collective-permute-start(s32[4,56,512]{2,1,0:T(8,128)S(1)} %pad_add_fusion.9), channel_id=1, source_target_pairs={{16,0},{32,16},{48,32},{64,48},{80,64},{96,80},{112,96},{17,1},{33... | collective-permute-start | bytes 1376264 | tf_op jit(solution)/shard_map/ppermute | solution.py:21
  149.5 4.2 %collective-permute-done.8 = s32[4,56,512]{2,1,0:T(8,128)S(1)} collective-permute-done((s32[4,56,512]{2,1,0:T(8,128)S(1)}, s32[4,56,512]{2,1,0:T(8,128)S(1)}, u32[]{:S(2)}, u32[]{:S(2)}) %collective-permute-start.8) | collective-permute-done | bytes 458784 | tf_op jit(solution)/shard_map/ppermute | solution.py:21
  153.7 5.6 %collective-permute-done.9 = s32[4,56,512]{2,1,0:T(8,128)S(1)} collective-permute-done((s32[4,56,512]{2,1,0:T(8,128)S(1)}, s32[4,56,512]{2,1,0:T(8,128)S(1)}, u32[]{:S(2)}, u32[]{:S(2)}) %collective-permute-start.9) | collective-permute-done | bytes 458784 | tf_op jit(solution)/shard_map/ppermute | solution.py:21
  160.3 5.8 %rows2.1.refs_2_ = s32[8,80,512]{2,1,0:T(8,128)} custom-call(s32[3,16]{1,0:T(4,128)} %reshape.59.refs_1_.refs_0_, s32[8,64,512]{2,1,0:T(8,128)} %get-tuple-element.10.refs_1_, s32[8,8,512]{2,1,0:T(8,128)} %get-tuple-element.11.refs_2_, s32[8,56,512]{2,1,0:T(8,128)} %pad_add_fusion.4.refs_3_), custom_call_target="tpu_custom_call" | custom-call | tf_op jit(solution)/shard_map/rows2/pallas_call | solution.py:219
  167.4 8.6 %collective-permute-start.10 = (s32[4,80,384]{2,1,0:T(8,128)S(1)}, s32[4,80,384]{2,1,0:T(8,128)S(1)}, u32[]{:S(2)}, u32[]{:S(2)}) collective-permute-start(s32[4,80,384]{2,1,0:T(8,128)S(1)} %get-tuple-element.20), channel_id=1, source_target_pairs={{0,1},{1,2},{2,3},{3,4},{4,5},{5,6},{6,7},{7,8},{8,9},{9,10},{10,1... | collective-permute-start | bytes 1474568 | tf_op jit(solution)/shard_map/ppermute | solution.py:21
  177.9 3.8 %collective-permute-done.10 = s32[4,80,384]{2,1,0:T(8,128)S(1)} collective-permute-done((s32[4,80,384]{2,1,0:T(8,128)S(1)}, s32[4,80,384]{2,1,0:T(8,128)S(1)}, u32[]{:S(2)}, u32[]{:S(2)}) %collective-permute-start.10) | collective-permute-done | bytes 491552 | tf_op jit(solution)/shard_map/ppermute | solution.py:21
  181.7 9.5 %collective-permute-done.11 = s32[4,80,384]{2,1,0:T(8,128)S(1)} collective-permute-done((s32[4,80,384]{2,1,0:T(8,128)S(1)}, s32[4,80,384]{2,1,0:T(8,128)S(1)}, u32[]{:S(2)}, u32[]{:S(2)}) %collective-permute-start.11) | collective-permute-done | bytes 491552 | tf_op jit(solution)/shard_map/ppermute | solution.py:21
  192.2 11.7 %night2.1 = (s32[8,64,512]{2,1,0:T(8,128)}, s32[8,8,512]{2,1,0:T(8,128)}) custom-call(f32[4,18]{1,0:T(4,128)} %pad_maximum_fusion.6.refs_0_, s32[3,16]{1,0:T(4,128)} %reshape.59.refs_1_.refs_0_, s32[8,80,512]{2,1,0:T(8,128)} %rows2.1.refs_2_, s32[8,80,384]{2,1,0:T(8,128)} %bitcast.57, f32[32,64,512]{2,1,0:T(8,128)} %conv.1.refs_4_, s32[32,64,512]{2,1,0:T(8,128)} %bitcast.47), custom_call_target="tpu_custom_call" | custom-call | tf_op jit(solution)/shard_map/night2/pallas_call | solution.py:185
  208.1 3.4 %collective-permute-start.13 = (s32[4,56,512]{2,1,0:T(8,128)S(1)}, s32[4,56,512]{2,1,0:T(8,128)S(1)}, u32[]{:S(2)}, u32[]{:S(2)}) collective-permute-start(s32[4,56,512]{2,1,0:T(8,128)S(1)} %pad_add_fusion.11), channel_id=1, source_target_pairs={{16,0},{32,16},{48,32},{64,48},{80,64},{96,80},{112,96},{17,1},{33... | collective-permute-start | bytes 1376264 | tf_op jit(solution)/shard_map/ppermute | solution.py:21
  211.4 3.9 %collective-permute-done.12 = s32[4,56,512]{2,1,0:T(8,128)S(1)} collective-permute-done((s32[4,56,512]{2,1,0:T(8,128)S(1)}, s32[4,56,512]{2,1,0:T(8,128)S(1)}, u32[]{:S(2)}, u32[]{:S(2)}) %collective-permute-start.12) | collective-permute-done | bytes 458784 | tf_op jit(solution)/shard_map/ppermute | solution.py:21
  215.3 5.6 %collective-permute-done.13 = s32[4,56,512]{2,1,0:T(8,128)S(1)} collective-permute-done((s32[4,56,512]{2,1,0:T(8,128)S(1)}, s32[4,56,512]{2,1,0:T(8,128)S(1)}, u32[]{:S(2)}, u32[]{:S(2)}) %collective-permute-start.13) | collective-permute-done | bytes 458784 | tf_op jit(solution)/shard_map/ppermute | solution.py:21
  221.9 5.8 %rows3.1.refs_2_ = s32[8,80,512]{2,1,0:T(8,128)} custom-call(s32[3,16]{1,0:T(4,128)} %reshape.59.refs_1_.refs_0_, s32[8,64,512]{2,1,0:T(8,128)} %get-tuple-element.12.refs_1_, s32[8,8,512]{2,1,0:T(8,128)} %get-tuple-element.13.refs_2_, s32[8,56,512]{2,1,0:T(8,128)} %pad_add_fusion.5.refs_3_), custom_call_target="tpu_custom_call" | custom-call | tf_op jit(solution)/shard_map/rows3/pallas_call | solution.py:219
  229.0 7.3 %collective-permute-start.14 = (s32[4,80,384]{2,1,0:T(8,128)S(1)}, s32[4,80,384]{2,1,0:T(8,128)S(1)}, u32[]{:S(2)}, u32[]{:S(2)}) collective-permute-start(s32[4,80,384]{2,1,0:T(8,128)S(1)} %get-tuple-element.18), channel_id=1, source_target_pairs={{0,1},{1,2},{2,3},{3,4},{4,5},{5,6},{6,7},{7,8},{8,9},{9,10},{10,1... | collective-permute-start | bytes 1474568 | tf_op jit(solution)/shard_map/ppermute | solution.py:21
  238.2 3.8 %collective-permute-done.14 = s32[4,80,384]{2,1,0:T(8,128)S(1)} collective-permute-done((s32[4,80,384]{2,1,0:T(8,128)S(1)}, s32[4,80,384]{2,1,0:T(8,128)S(1)}, u32[]{:S(2)}, u32[]{:S(2)}) %collective-permute-start.14) | collective-permute-done | bytes 491552 | tf_op jit(solution)/shard_map/ppermute | solution.py:21
  242.0 8.3 %collective-permute-done.15 = s32[4,80,384]{2,1,0:T(8,128)S(1)} collective-permute-done((s32[4,80,384]{2,1,0:T(8,128)S(1)}, s32[4,80,384]{2,1,0:T(8,128)S(1)}, u32[]{:S(2)}, u32[]{:S(2)}) %collective-permute-start.15) | collective-permute-done | bytes 491552 | tf_op jit(solution)/shard_map/ppermute | solution.py:21
  251.4 10.7 %night3.1 = (f32[8,64,512]{2,1,0:T(8,128)}, f32[8,64,512]{2,1,0:T(8,128)}) custom-call(f32[4,18]{1,0:T(4,128)} %pad_maximum_fusion.6.refs_0_, s32[3,16]{1,0:T(4,128)} %reshape.59.refs_1_.refs_0_, s32[8,80,512]{2,1,0:T(8,128)} %rows3.1.refs_2_, s32[8,80,384]{2,1,0:T(8,128)} %bitcast.55, f32[32,64,512]{2,1,0:T(8,128)} %conv.1.refs_4_, s32[32,64,512]{2,1,0:T(8,128)} %bitcast.48), custom_call_target="tpu_custom_call" | custom-call | tf_op jit(solution)/shard_map/night3/pallas_call | solution.py:185
  (61 shorter events, 38.1 us)
Async XLA Ops:
  0.6 10.4 %copy-start = (bf16[4,8,21,21]{3,1,2,0:T(8,128)(2,1)S(1)}, bf16[4,8,21,21]{3,1,2,0:T(8,128)(2,1)}, u32[]{:S(2)}) copy-start(bf16[4,8,21,21]{3,1,2,0:T(8,128)(2,1)} %param.8) | copy-start | bytes 84676
  0.6 10.9 %copy-start.1 = (f32[4,8]{1,0:T(4,128)S(1)}, f32[4,8]{1,0:T(4,128)}, u32[]{:S(2)}) copy-start(f32[4,8]{1,0:T(4,128)} %param.10) | copy-start | bytes 388
  2.1 11.0 %copy-start.2 = (s32[3,8,2]{1,2,0:T(2,128)S(1)}, s32[3,8,2]{1,2,0:T(2,128)}, u32[]{:S(2)}) copy-start(s32[3,8,2]{1,2,0:T(2,128)} %param.11) | copy-start | bytes 580
  2.1 18.3 %collective-permute-start = (bf16[32,10,512]{2,1,0:T(8,128)(2,1)S(1)}, bf16[32,10,512]{2,1,0:T(8,128)(2,1)S(1)}, u32[]{:S(2)}, u32[]{:S(2)}) collective-permute-start(bf16[32,10,512]{2,1,0:T(8,128)(2,1)S(1)} %get-tuple-element.16), channel_id=1, source_target_pairs={{16,0},{32,16},{48,32},{64,48},{80,64},{96,80},{112,96},{17,1},{33... | collective-permute-start | bytes 983048 | tf_op jit(solution)/shard_map/ppermute | solution.py:21
  4.1 17.2 %collective-permute-start.1 = (bf16[32,10,512]{2,1,0:T(8,128)(2,1)S(1)}, bf16[32,10,512]{2,1,0:T(8,128)(2,1)}, u32[]{:S(2)}, u32[]{:S(2)}) collective-permute-start(bf16[32,10,512]{2,1,0:T(8,128)(2,1)S(1)} %get-tuple-element.17), channel_id=1, source_target_pairs={{0,16},{16,32},{32,48},{48,64},{64,80},{80,96},{96,112},{1,17},{17... | collective-permute-start | bytes 983048 | tf_op jit(solution)/shard_map/ppermute | solution.py:21
  26.2 7.8 %collective-permute-start.2 = (bf16[32,128,10]{1,0,2:T(8,128)(2,1)S(1)}, bf16[32,128,10]{1,0,2:T(8,128)(2,1)S(1)}, u32[]{:S(2)}, u32[]{:S(2)}) collective-permute-start(bf16[32,128,10]{1,0,2:T(8,128)(2,1)S(1)} %copy.32), channel_id=1, source_target_pairs={{1,0},{2,1},{3,2},{4,3},{5,4},{6,5},{7,6},{8,7},{9,8},{10,9},{11,1... | collective-permute-start | bytes 245768 | tf_op jit(solution)/shard_map/ppermute | solution.py:21
  30.4 4.5 %collective-permute-start.3 = (bf16[32,128,10]{1,0,2:T(8,128)(2,1)S(1)}, bf16[32,128,10]{1,0,2:T(8,128)(2,1)S(1)}, u32[]{:S(2)}, u32[]{:S(2)}) collective-permute-start(bf16[32,128,10]{1,0,2:T(8,128)(2,1)S(1)} %copy.33), channel_id=1, source_target_pairs={{0,1},{1,2},{2,3},{3,4},{4,5},{5,6},{6,7},{7,8},{8,9},{9,10},{10,1... | collective-permute-start | bytes 245768 | tf_op jit(solution)/shard_map/ppermute | solution.py:21
  84.0 17.7 %collective-permute-start.4 = (s32[4,56,512]{2,1,0:T(8,128)S(1)}, s32[4,56,512]{2,1,0:T(8,128)S(1)}, u32[]{:S(2)}, u32[]{:S(2)}) collective-permute-start(s32[4,56,512]{2,1,0:T(8,128)S(1)} %pad_add_fusion.6), channel_id=1, source_target_pairs={{0,16},{16,32},{32,48},{48,64},{64,80},{80,96},{96,112},{1,17},{17... | collective-permute-start | bytes 1376264 | tf_op jit(solution)/shard_map/ppermute | solution.py:21
  92.5 17.0 %collective-permute-start.5 = (s32[4,56,512]{2,1,0:T(8,128)S(1)}, s32[4,56,512]{2,1,0:T(8,128)S(1)}, u32[]{:S(2)}, u32[]{:S(2)}) collective-permute-start(s32[4,56,512]{2,1,0:T(8,128)S(1)} %pad_add_fusion.7), channel_id=1, source_target_pairs={{16,0},{32,16},{48,32},{64,48},{80,64},{96,80},{112,96},{17,1},{33... | collective-permute-start | bytes 1376264 | tf_op jit(solution)/shard_map/ppermute | solution.py:21
  117.6 11.7 %collective-permute-start.7 = (s32[4,80,384]{2,1,0:T(8,128)S(1)}, s32[4,80,384]{2,1,0:T(8,128)S(1)}, u32[]{:S(2)}, u32[]{:S(2)}) collective-permute-start(s32[4,80,384]{2,1,0:T(8,128)S(1)} %get-tuple-element.23), channel_id=1, source_target_pairs={{1,0},{2,1},{3,2},{4,3},{5,4},{6,5},{7,6},{8,7},{9,8},{10,9},{11,1... | collective-permute-start | bytes 1474568 | tf_op jit(solution)/shard_map/ppermute | solution.py:21
  119.5 9.8 %collective-permute-start.6 = (s32[4,80,384]{2,1,0:T(8,128)S(1)}, s32[4,80,384]{2,1,0:T(8,128)S(1)}, u32[]{:S(2)}, u32[]{:S(2)}) collective-permute-start(s32[4,80,384]{2,1,0:T(8,128)S(1)} %get-tuple-element.22), channel_id=1, source_target_pairs={{0,1},{1,2},{2,3},{3,4},{4,5},{5,6},{6,7},{7,8},{8,9},{9,10},{10,1... | collective-permute-start | bytes 1474568 | tf_op jit(solution)/shard_map/ppermute | solution.py:21
  144.2 9.5 %collective-permute-start.8 = (s32[4,56,512]{2,1,0:T(8,128)S(1)}, s32[4,56,512]{2,1,0:T(8,128)S(1)}, u32[]{:S(2)}, u32[]{:S(2)}) collective-permute-start(s32[4,56,512]{2,1,0:T(8,128)S(1)} %pad_add_fusion.8), channel_id=1, source_target_pairs={{0,16},{16,32},{32,48},{48,64},{64,80},{80,96},{96,112},{1,17},{17... | collective-permute-start | bytes 1376264 | tf_op jit(solution)/shard_map/ppermute | solution.py:21
  146.4 12.8 %collective-permute-start.9 = (s32[4,56,512]{2,1,0:T(8,128)S(1)}, s32[4,56,512]{2,1,0:T(8,128)S(1)}, u32[]{:S(2)}, u32[]{:S(2)}) collective-permute-start(s32[4,56,512]{2,1,0:T(8,128)S(1)} %pad_add_fusion.9), channel_id=1, source_target_pairs={{16,0},{32,16},{48,32},{64,48},{80,64},{96,80},{112,96},{17,1},{33... | collective-permute-start | bytes 1376264 | tf_op jit(solution)/shard_map/ppermute | solution.py:21
  167.4 14.4 %collective-permute-start.10 = (s32[4,80,384]{2,1,0:T(8,128)S(1)}, s32[4,80,384]{2,1,0:T(8,128)S(1)}, u32[]{:S(2)}, u32[]{:S(2)}) collective-permute-start(s32[4,80,384]{2,1,0:T(8,128)S(1)} %get-tuple-element.20), channel_id=1, source_target_pairs={{0,1},{1,2},{2,3},{3,4},{4,5},{5,6},{6,7},{7,8},{8,9},{9,10},{10,1... | collective-permute-start | bytes 1474568 | tf_op jit(solution)/shard_map/ppermute | solution.py:21
  176.0 15.2 %collective-permute-start.11 = (s32[4,80,384]{2,1,0:T(8,128)S(1)}, s32[4,80,384]{2,1,0:T(8,128)S(1)}, u32[]{:S(2)}, u32[]{:S(2)}) collective-permute-start(s32[4,80,384]{2,1,0:T(8,128)S(1)} %get-tuple-element.21), channel_id=1, source_target_pairs={{1,0},{2,1},{3,2},{4,3},{5,4},{6,5},{7,6},{8,7},{9,8},{10,9},{11,1... | collective-permute-start | bytes 1474568 | tf_op jit(solution)/shard_map/ppermute | solution.py:21
  206.1 9.2 %collective-permute-start.12 = (s32[4,56,512]{2,1,0:T(8,128)S(1)}, s32[4,56,512]{2,1,0:T(8,128)S(1)}, u32[]{:S(2)}, u32[]{:S(2)}) collective-permute-start(s32[4,56,512]{2,1,0:T(8,128)S(1)} %pad_add_fusion.10), channel_id=1, source_target_pairs={{0,16},{16,32},{32,48},{48,64},{64,80},{80,96},{96,112},{1,17},{17... | collective-permute-start | bytes 1376264 | tf_op jit(solution)/shard_map/ppermute | solution.py:21
  208.1 12.8 %collective-permute-start.13 = (s32[4,56,512]{2,1,0:T(8,128)S(1)}, s32[4,56,512]{2,1,0:T(8,128)S(1)}, u32[]{:S(2)}, u32[]{:S(2)}) collective-permute-start(s32[4,56,512]{2,1,0:T(8,128)S(1)} %pad_add_fusion.11), channel_id=1, source_target_pairs={{16,0},{32,16},{48,32},{64,48},{80,64},{96,80},{112,96},{17,1},{33... | collective-permute-start | bytes 1376264 | tf_op jit(solution)/shard_map/ppermute | solution.py:21
  229.0 13.0 %collective-permute-start.14 = (s32[4,80,384]{2,1,0:T(8,128)S(1)}, s32[4,80,384]{2,1,0:T(8,128)S(1)}, u32[]{:S(2)}, u32[]{:S(2)}) collective-permute-start(s32[4,80,384]{2,1,0:T(8,128)S(1)} %get-tuple-element.18), channel_id=1, source_target_pairs={{0,1},{1,2},{2,3},{3,4},{4,5},{5,6},{6,7},{7,8},{8,9},{9,10},{10,1... | collective-permute-start | bytes 1474568 | tf_op jit(solution)/shard_map/ppermute | solution.py:21
  236.3 14.1 %collective-permute-start.15 = (s32[4,80,384]{2,1,0:T(8,128)S(1)}, s32[4,80,384]{2,1,0:T(8,128)S(1)}, u32[]{:S(2)}, u32[]{:S(2)}) collective-permute-start(s32[4,80,384]{2,1,0:T(8,128)S(1)} %get-tuple-element.19), channel_id=1, source_target_pairs={{1,0},{2,1},{3,2},{4,3},{5,4},{6,5},{7,6},{8,7},{9,8},{10,9},{11,1... | collective-permute-start | bytes 1474568 | tf_op jit(solution)/shard_map/ppermute | solution.py:21

commit v2 on v0

v2 whole, which is shorter than its diff:
```python
import jax
import jax.numpy as jnp
from jax import lax
from jax.experimental import pallas as pl
from jax.experimental.pallas import tpu as pltpu
from jax.sharding import PartitionSpec as P

f32, bf16, i32 = jnp.float32, jnp.bfloat16, jnp.int32
band_scale = 1.5
weight_floor = 1.0
ROWS, COLS = 64, 512
MR, MC = 48, 384
PLANES, NIGHTS, EXPS, KS, RAD = 8, 4, 8, 21, 10
NEXP = NIGHTS * EXPS
STEP = 16
LAG = 2
MESH = pl.DeviceIdType.MESH


def whole_kernel(table, offs, e_hbm, kv, masks_hbm, flux_hbm, weight_hbm, oflux_hbm, oweight_hbm, *scratch):
    (z, masks, flux0, weight0, filt, taps, wins, hs, hr, fbuf, wbuf, sb, rext, cext, of, ow,
     in_sem, out_sem, rh_s, rh_r, ch_s, ch_r, row_s, row_r, col_s, col_r) = scratch
    sy, sx = lax.axis_index("sy"), lax.axis_index("sx")
    ny, nx = lax.axis_size("sy"), lax.axis_size("sx")
    has = {"up": sy > 0, "down": sy < ny - 1, "left": sx > 0, "right": sx < nx - 1}
    dev = {"up": (sy - 1, sx), "down": (sy + 1, sx), "left": (sy, sx - 1), "right": (sy, sx + 1)}
    back = {"up": "down", "down": "up", "left": "right", "right": "left"}

    def remote(src, dst, ss, rs, to):
        return pltpu.make_async_remote_copy(
            src_ref=src, dst_ref=dst, send_sem=ss, recv_sem=rs, device_id=dev[to], device_id_type=MESH
        )

    def row_halo(n, to):
        k = 0 if to == "up" else 1
        first, land = (0, 64) if to == "up" else (48, 80)
        some = pl.ds(n * EXPS, EXPS)
        return remote(z.at[some, pl.ds(first, 16)], z.at[some, pl.ds(land, 16)], rh_s.at[n, k], rh_r.at[n, k], to)

    def col_halo(n, to):
        k = 0 if to == "left" else 1
        return remote(hs.at[n, k], hr.at[n, k], ch_s.at[n, k], ch_r.at[n, k], to)

    def row_copy(n, p, to):
        first, land = (8, 0) if to == "down" else (0, 64)
        return remote(sb.at[n, p, pl.ds(first, 56)], rext.at[n, p, pl.ds(land, 56)], row_s.at[n, p], row_r.at[n, p], to)

    def col_copy(n, p, to):
        first, land = (COLS, 0) if to == "right" else (0, COLS)
        return remote(cext.at[n, p, :, pl.ds(first, MC)], cext.at[n, p, :, pl.ds(land, MC)], col_s.at[n, p], col_r.at[n, p], to)

    def go(cond, copy, to, what):
        there = has[back[to]] if what == "wait_recv" else has[to]

        @pl.when(jnp.logical_and(cond, there))
        def _():
            getattr(copy(to), what)()

    def rows_go(n, p, what):
        go(p < 4, lambda to: row_copy(n, p, to), "down", what)
        go(p >= 4, lambda to: row_copy(n, p, to), "up", what)

    def cols_go(n, p, what):
        go(p % 2 == 0, lambda to: col_copy(n, p, to), "right", what)
        go(p % 2 == 1, lambda to: col_copy(n, p, to), "left", what)

    def halo_go(kind, n, sides, what):
        for to in sides:
            go(True, lambda to: kind(n, to), to, what)

    copies = [
        pltpu.make_async_copy(e_hbm, z.at[:, pl.ds(0, ROWS)], in_sem.at[0]),
        pltpu.make_async_copy(flux_hbm, flux0, in_sem.at[1]),
        pltpu.make_async_copy(weight_hbm, weight0, in_sem.at[2]),
        pltpu.make_async_copy(masks_hbm, masks, in_sem.at[3]),
    ]
    for c in copies:
        c.start()

    def clear(n, c):
        z[n, ROWS:, :] = jnp.zeros((32, COLS), bf16)
        return c

    lax.fori_loop(0, NEXP, clear, 0)
    for n in range(NIGHTS):
        hr[n] = jnp.zeros((2, 96, 128), bf16)

    def clear_planes(p, c):
        for n in range(NIGHTS - 1):
            rext[n, p, 0:56, :] = jnp.zeros((56, COLS), i32)
            rext[n, p, 64:120, :] = jnp.zeros((56, COLS), i32)
            cext[n, p, :, 0:MC] = jnp.zeros((80, MC), i32)
            cext[n, p, :, COLS:1024] = jnp.zeros((80, 512), i32)
        return c

    lax.fori_loop(0, PLANES, clear_planes, 0)
    taps[...] = jnp.zeros_like(taps)
    wins[...] = jnp.zeros_like(wins)

    barrier = pltpu.get_barrier_semaphore()
    for to in dev:
        @pl.when(has[to])
        def _():
            pl.semaphore_signal(barrier, inc=1, device_id=dev[to], device_id_type=MESH)
    pl.semaphore_wait(barrier, sum(jnp.where(has[to], 1, 0) for to in dev))

    copies[0].wait()
    halo_go(row_halo, 0, ("up", "down"), "start")
    halo_go(row_halo, 1, ("up", "down"), "start")

    lane = lax.broadcasted_iota(i32, (96, 128), 1)

    def col_halo_send(n):
        def put(j, c):
            to_left, to_right = c
            first, last = z[n * EXPS + j, :, 0:128], z[n * EXPS + j, :, 384:512]
            here = (lane >= 10 * j) & (lane < 10 * j + 10)
            to_left = jnp.where(here, pltpu.roll(first.astype(f32), 10 * j, 1), to_left)
            to_right = jnp.where(here, pltpu.roll(last.astype(f32), (10 * j + 10) % 128, 1), to_right)
            return to_left, to_right

        zero = jnp.zeros((96, 128), f32)
        to_left, to_right = lax.fori_loop(0, EXPS, put, (zero, zero))
        hs[n, 0] = to_left.astype(bf16)
        hs[n, 1] = to_right.astype(bf16)
        halo_go(col_halo, n, ("left", "right"), "start")

    def conv(n, j):
        k = n * EXPS + j
        for b in range(KS):
            b0, ph = b // 4, b % 4
            base = jnp.broadcast_to(kv[k, b : b + 1, :], (ROWS, 128))
            t = pltpu.roll(base, 0, 1, stride=1, stride_axis=0)
            taps[ph * 64 : (ph + 1) * 64, b0 * 128 : (b0 + 1) * 128] = t.astype(bf16)
        right = pltpu.roll(hr[n, 0].astype(f32), (128 - 10 * j) % 128, 1)
        left = pltpu.roll(hr[n, 1].astype(f32), (246 - 10 * j) % 128, 1)
        edge = jnp.where(lane < 10, right, jnp.where(lane >= 118, left, 0.0)).astype(bf16)
        tile = jnp.concatenate([z[k], edge], axis=1)
        for b0 in range(6):
            w = pltpu.roll(tile, (RAD - 4 * b0) % 640, 1)
            wins[b0 * 128 : b0 * 128 + 80, :] = w[:80]
            wins[b0 * 128 + 112 : b0 * 128 + 128, :] = w[80:]
        acc = jnp.dot(taps[...], wins[...], preferred_element_type=f32)
        out = acc[0:64, 0:COLS]
        for ph in range(1, 4):
            out = out + pltpu.roll(acc[ph * 64 : (ph + 1) * 64, :], 640 - ph, 1)[:, :COLS]
        filt[k] = out

    def conv_range(n, a, b):
        def one(j, c):
            conv(n, j)
            return c

        lax.fori_loop(a, b, one, 0)

    lane_row = lax.broadcasted_iota(i32, (STEP, COLS), 0)

    def bits(amount, bit, shape):
        return (jnp.full(shape, amount, i32) & bit) != 0

    def accumulate(n, p):
        first, final = n == 0, n == NIGHTS - 1
        bit = jnp.left_shift(jnp.int32(1), p)
        if not first:
            row_off = offs[n - 1, 2 * p]
            col_off = offs[n - 1, 2 * p + 1]
            start = jnp.where(p % 2 == 0, MC - col_off, -col_off)
            turn = (640 - (start & 127)) % 640

            def window(rows):
                x = cext[n - 1, p, rows, :]
                x = jnp.where(bits(start, 256, (x.shape[0], 768)), x[:, 256:], x[:, :768])
                x = jnp.where(bits(start, 128, (x.shape[0], 640)), x[:, 128:], x[:, :640])
                return pltpu.roll(x, turn, 1)[:, :COLS]

            own_gain = jnp.exp2(window(pl.ds(64, 8)).astype(f32) * 0.25) * (1.0 / 32766.0)
            far_gain = jnp.exp2(window(pl.ds(72, 8)).astype(f32) * 0.25) * (1.0 / 32766.0)
            own_gain = jnp.concatenate([own_gain, own_gain], axis=0)
            far_gain = jnp.concatenate([far_gain, far_gain], axis=0)
            dec = table[n, 2 * EXPS]
            lo = jnp.where(p < 4, row_off, 0)
            hi = jnp.where(p < 4, ROWS, ROWS + row_off)

        def step(i, peak):
            rows = pl.ds(pl.multiple_of(i * STEP, STEP), STEP)
            if first:
                flux, weight = flux0[p, rows, :], weight0[p, rows, :]
            else:
                packed = window(rows)
                y = lane_row + i * STEP
                gain = jnp.where((y >= lo) & (y < hi), own_gain, far_gain)
                flux = (packed >> 16).astype(f32) * gain
                weight = (packed & 0xFFFF).astype(f32) * dec
            for e in range(EXPS):
                wv = table[n, e]
                half = table[n, EXPS + e]
                filtered = filt[n * EXPS + e, rows, :]
                mask = masks[n * EXPS + e, rows, :]
                mean = flux / jnp.maximum(weight, weight_floor)
                clipped = jnp.clip(filtered, mean - half, mean + half)
                chosen = jnp.where((mask & bit) != 0, clipped, filtered)
                flux = flux + wv * chosen
                weight = weight + wv
            if final:
                of[p, rows, :] = flux
                ow[p, rows, :] = weight
                return peak
            fbuf[rows, :] = flux
            wbuf[rows, :] = weight
            size = jnp.abs(flux)
            return jnp.maximum(peak, jnp.maximum(size[:8], size[8:]))

        peak = lax.fori_loop(0, ROWS // STEP, step, jnp.zeros((8, COLS), f32))
        if final:
            return
        for k in (4, 2, 1):
            peak = jnp.maximum(peak, pltpu.roll(peak, k, 0))
        expo = jnp.ceil(4.0 * jnp.log2(jnp.maximum(peak, 1e-30)) + 0.01)
        gain = jnp.exp2(expo * -0.25) * 32766.0
        enc = table[n, 2 * EXPS + 1]
        base = jnp.where(p < 4, 56, 0)

        def pack(i, c):
            rows = pl.ds(pl.multiple_of(i * 8, 8), 8)
            q = jnp.round(fbuf[rows, :] * gain).astype(i32)
            w = (wbuf[rows, :] * enc + 0.5).astype(i32)
            both = (q << 16) | w
            sb[n, p, rows, :] = both
            rext[n, p, pl.ds(pl.multiple_of(base + i * 8, 8), 8), :] = both
            return c

        lax.fori_loop(0, ROWS // 8, pack, 0)
        sb[n, p, pl.ds(pl.multiple_of(jnp.where(p < 4, 8, 48), 8), 8), :] = expo.astype(i32)
        rows_go(n, p, "start")

    def shift_rows(n, p):
        rows_go(n, p, "wait_recv")
        row_off = offs[n, 2 * p]
        start = jnp.where(p < 4, 8 + MR - row_off, -row_off)
        lanes = pl.ds(pl.multiple_of(jnp.where(p % 2 == 0, MC, 0), 128), COLS)
        x = rext[n, p]
        x = jnp.concatenate([jnp.where(bits(start, 32, (88, COLS)), x[32:], x[:88]), x[88:96]], axis=0)
        x = jnp.where(bits(start, 16, (80, COLS)), x[16:], x[:80])
        x = jnp.where(bits(start, 8, (72, COLS)), x[8:], x[:72])
        moved = pltpu.roll(x, (72 - (start & 7)) % 72, 0)[:ROWS]
        own = sb[n, p, pl.ds(pl.multiple_of(jnp.where(p < 4, 8, 48), 8), 8), :]
        far = rext[n, p, pl.ds(pl.multiple_of(jnp.where(p < 4, 0, 112), 8), 8), :]
        cext[n, p, 0:ROWS, lanes] = moved
        cext[n, p, ROWS : ROWS + 8, lanes] = own
        cext[n, p, ROWS + 8 :, lanes] = far
        cols_go(n, p, "start")

    def plane_at(i):
        return (i * 5) % PLANES

    halo_go(row_halo, 0, ("up", "down"), "wait_recv")
    col_halo_send(0)
    for n in range(2, NIGHTS):
        halo_go(row_halo, n, ("up", "down"), "start")
    halo_go(col_halo, 0, ("left", "right"), "wait_recv")
    conv_range(0, 0, EXPS)
    for c in copies[1:]:
        c.wait()
    for n in range(1, NIGHTS):
        halo_go(row_halo, n, ("up", "down"), "wait_recv")
        col_halo_send(n)

    for n in range(NIGHTS):
        if n + 1 < NIGHTS:
            def body(i, c):
                p = plane_at(i)
                if n > 0:
                    cols_go(n - 1, p, "wait_recv")
                accumulate(n, p)

                @pl.when(i >= LAG)
                def _():
                    shift_rows(n, plane_at(i - LAG))
                    conv(n + 1, i - LAG)

                return c

            halo_go(col_halo, n + 1, ("left", "right"), "wait_recv")
            lax.fori_loop(0, PLANES, body, 0)

            def tail(i, c):
                shift_rows(n, plane_at(i))
                conv(n + 1, i)
                return c

            lax.fori_loop(PLANES - LAG, PLANES, tail, 0)
        else:
            def out_copies(p):
                return (
                    pltpu.make_async_copy(of.at[p], oflux_hbm.at[p], out_sem.at[0, p]),
                    pltpu.make_async_copy(ow.at[p], oweight_hbm.at[p], out_sem.at[1, p]),
                )

            def last(i, c):
                p = plane_at(i)
                cols_go(n - 1, p, "wait_recv")
                accumulate(n, p)
                for d in out_copies(p):
                    d.start()
                return c

            lax.fori_loop(0, PLANES, last, 0)

    def finish(p, c):
        for d in out_copies(p):
            d.wait()
        for n in range(NIGHTS - 1):
            rows_go(n, p, "wait_send")
            cols_go(n, p, "wait_send")
        return c

    lax.fori_loop(0, PLANES, finish, 0)
    for n in range(NIGHTS):
        halo_go(row_halo, n, ("up", "down"), "wait_send")
        halo_go(col_halo, n, ("left", "right"), "wait_send")


def whole_call(table, offsets, e, kv, masks, flux, weight):
    anywhere = pl.BlockSpec(memory_space=pl.ANY)
    smem = pl.BlockSpec(memory_space=pltpu.SMEM)
    dma = pltpu.SemaphoreType.DMA
    n = NIGHTS - 1
    vm = pltpu.VMEM
    return pl.pallas_call(
        whole_kernel,
        in_specs=[smem, smem, anywhere, pl.BlockSpec(memory_space=pltpu.VMEM), anywhere, anywhere, anywhere],
        out_specs=[anywhere, anywhere],
        out_shape=[jax.ShapeDtypeStruct((PLANES, ROWS, COLS), f32)] * 2,
        scratch_shapes=[
            vm((NEXP, 96, COLS), bf16),
            vm((NEXP, ROWS, COLS), i32),
            vm((PLANES, ROWS, COLS), f32),
            vm((PLANES, ROWS, COLS), f32),
            vm((NEXP, ROWS, COLS), f32),
            vm((256, 768), bf16),
            vm((768, 640), bf16),
            vm((NIGHTS, 2, 96, 128), bf16),
            vm((NIGHTS, 2, 96, 128), bf16),
            vm((ROWS, COLS), f32),
            vm((ROWS, COLS), f32),
            vm((n, PLANES, ROWS, COLS), i32),
            vm((n, PLANES, 120, COLS), i32),
            vm((n, PLANES, 80, 1024), i32),
            vm((PLANES, ROWS, COLS), f32),
            vm((PLANES, ROWS, COLS), f32),
            dma((4,)), dma((2, PLANES)),
            dma((NIGHTS, 2)), dma((NIGHTS, 2)), dma((NIGHTS, 2)), dma((NIGHTS, 2)),
            dma((n, PLANES)), dma((n, PLANES)), dma((n, PLANES)), dma((n, PLANES)),
        ],
        compiler_params=pltpu.CompilerParams(collective_id=0, has_side_effects=True, vmem_limit_bytes=60 << 20),
        name="stack",
    )(table, offsets, e, kv, masks, flux, weight)


def scalar_table(exposure_weights):
    totals = 4.0 + jnp.cumsum(jnp.sum(exposure_weights, axis=1))
    top = totals * 1.0001
    enc = 65535.0 / top
    dec = jnp.concatenate([jnp.ones((1,), f32), top[:-1] / 65535.0])
    half = band_scale / jnp.sqrt(exposure_weights)
    return jnp.concatenate([exposure_weights, half, dec[:, None], enc[:, None]], axis=1)


def kernel_rows(psf_kernels):
    k = psf_kernels.astype(f32).reshape(NEXP, KS, KS).transpose(0, 2, 1)
    gap = jnp.zeros((NEXP, KS, 128 - KS), f32)
    k = jnp.concatenate([k[:, :, RAD:], gap, k[:, :, :RAD]], axis=2)
    return jnp.pad(k, ((0, 0), (0, 3), (0, 0)))


def per_device(exposures, psf_kernels, clip_masks, exposure_weights, plane_offsets, flux, weight):
    e = exposures.reshape(NEXP, ROWS, COLS)
    masks = clip_masks.reshape(NEXP, ROWS, COLS)
    table = scalar_table(exposure_weights)
    offsets = plane_offsets.reshape(NIGHTS - 1, 2 * PLANES)
    return tuple(whole_call(table, offsets, e, kernel_rows(psf_kernels), masks, flux, weight))


def solution(mesh):
    return jax.shard_map(
        per_device,
        mesh=mesh,
        in_specs=(
            P(None, None, "sy", "sx"),
            P(),
            P(None, None, "sy", "sx"),
            P(),
            P(),
            P(None, "sy", "sx"),
            P(None, "sy", "sx"),
        ),
        out_specs=(P(None, "sy", "sx"), P(None, "sy", "sx")),
        check_vma=False,
    )
```

time: 1690 us -> 128 us (0.08)
  the two profiles are of different devices: /device:TPU:120 before, /device:TPU:22 now
where the time goes in v2:
time: 128 us
  Pallas kernels  116 us (91%)
  local copies, waits for them, and re-layouts  8.41 us (7%)
  other arithmetic  2.56 us (2%)
    pallas_call x1, Pallas kernels, whole_call(): pl.pallas_call(whole_kernel, in_specs=[smem, smem, anywhere, pl.BlockSpec...  116 us
    unnamed x3, local copies, waits for them, and re-layouts  5.29 us

profile of v2, /device:TPU:22, one launch (start us, length us, event | category | flops | bytes accessed | tf_op | source)
XLA Modules:
  0.0 128.1 jit_solution(3760724409280325457)
XLA Ops:
  0.6 0.1 pad.6.clone
  0.7 0.8 rsqrt_multiply_fusion
  1.5 0.1 copy.13
  1.7 0.1 multiply_reduce_fusion
  1.8 0.1 maximum_bitcast_fusion
  1.9 0.1 copy.14
  2.0 1.3 %pad_maximum_fusion.1.table = f32[4,18]{1,0:T(4,128)} fusion(f32[4,1]{1,0:T(4,128)S(1)} %get-tuple-element.5, f32[4,1]{1,0:T(4,128)S(1)} %copy.14, f32[4,8]{1,0:T(4,128)S(1)} %get-tuple-element.2, f32[4,8]{1,0:T(4,128)} %param.10), kind=kLoop, calls=%fused_computation.1 | loop fusion | flops 216 | bytes 576 | tf_op jit(solution)/shard_map/concatenate | solution.py:366
  3.3 0.8 copy.15
  4.1 0.7 reshape.41.offs
  4.7 1.2 copy.16
  6.0 0.2 slice.13
  6.1 0.2 pad_maximum_fusion
  6.3 0.8 pad.4.kv
  7.1 116.4 %stack.1 = (f32[8,64,512]{2,1,0:T(8,128)}, f32[8,64,512]{2,1,0:T(8,128)}) custom-call(f32[4,18]{1,0:T(4,128)} %pad_maximum_fusion.1.table, s32[3,16]{1,0:T(4,128)} %reshape.41.offs, bf16[32,64,512]{2,1,0:T(8,128)(2,1)} %bitcast.12, f32[32,24,128]{2,1,0:T(8,128)} %pad.4.kv, s32[32,64,512]{2,1,0:T(8,128)} %bitcast.9, f32[8,64,512]{2,1,0:T(8,128)} %flux_hbm.1, ...), custom_call_target="tpu_custom_call" | custom-call | tf_op jit(solution)/shard_map/stack/pallas_call | solution.py:329
  123.5 2.3 %copy.19 = f32[8,64,512]{2,1,0:T(8,128)} copy(f32[8,64,512]{2,1,0:T(8,128)} %get-tuple-element.8) | data formatting | bytes 2097152
  125.8 2.3 %copy.20 = f32[8,64,512]{2,1,0:T(8,128)} copy(f32[8,64,512]{2,1,0:T(8,128)} %get-tuple-element.9) | data formatting | bytes 2097152
  (3 shorter events, 0.1 us)

commit v3 on v2

--- a/solution.py
+++ b/solution.py
@@ -13,17 +13,22 @@
 PLANES, NIGHTS, EXPS, KS, RAD = 8, 4, 8, 21, 10
 NEXP = NIGHTS * EXPS
 STEP = 16
-LAG = 2
+LAG = 3
+ORDER = (2, 7, 0, 5, 3, 6, 1, 4)
 MESH = pl.DeviceIdType.MESH
 
 
-def whole_kernel(table, offs, e_hbm, kv, masks_hbm, flux_hbm, weight_hbm, oflux_hbm, oweight_hbm, *scratch):
-    (z, masks, flux0, weight0, filt, taps, wins, hs, hr, fbuf, wbuf, sb, rext, cext, of, ow,
-     in_sem, out_sem, rh_s, rh_r, ch_s, ch_r, row_s, row_r, col_s, col_r) = scratch
+def whole_kernel(gains, offs, e_hbm, kv, masks_hbm, flux_hbm, weight_hbm, oflux_hbm, oweight_hbm, *scratch):
+    (z, masks, flux0, weight0, filt, taps, wins, hs, hr, fbuf, wbuf, sb, rext, cext, rl, of, ow,
+     in_sem, out_sem, rh_s, rh_r, ch_s, ch_r, row_s, row_r, col_s, col_r, rl_s, rl_r) = scratch
     sy, sx = lax.axis_index("sy"), lax.axis_index("sx")
     ny, nx = lax.axis_size("sy"), lax.axis_size("sx")
     has = {"up": sy > 0, "down": sy < ny - 1, "left": sx > 0, "right": sx < nx - 1}
     dev = {"up": (sy - 1, sx), "down": (sy + 1, sx), "left": (sy, sx - 1), "right": (sy, sx + 1)}
+    mid = ny // 2
+    relays = ny == 8
+    first_hop = {"down": (mid - 1, 0), "up": (mid, ny - 1)}
+    last_hop = {"down": (0, mid), "up": (ny - 1, mid - 1)}
     back = {"up": "down", "down": "up", "left": "right", "right": "left"}
 
     def remote(src, dst, ss, rs, to):
@@ -56,9 +61,42 @@
         def _():
             getattr(copy(to), what)()
 
+    def remote_to(src, dst, ss, rs, row):
+        return pltpu.make_async_remote_copy(
+            src_ref=src, dst_ref=dst, send_sem=ss, recv_sem=rs, device_id=(row, sx), device_id_type=MESH
+        )
+
+    def relay_in(n, p, to):
+        first = 8 if to == "down" else 0
+        k = p % 2
+        return remote_to(sb.at[n, p, pl.ds(first, 56)], rl.at[n, k], row_s.at[n, p], rl_r.at[n, k], first_hop[to][1])
+
+    def relay_out(n, p, to):
+        land = 0 if to == "down" else 64
+        k = p % 2
+        return remote_to(rl.at[n, k], rext.at[n, p, pl.ds(land, 56)], rl_s.at[n, k], row_r.at[n, p], last_hop[to][1])
+
     def rows_go(n, p, what):
-        go(p < 4, lambda to: row_copy(n, p, to), "down", what)
-        go(p >= 4, lambda to: row_copy(n, p, to), "up", what)
+        for to, mine in (("down", p < 4), ("up", p >= 4)):
+            if relays and what != "wait_recv":
+                around = mine & (p % 4 >= 2) & (sy == first_hop[to][0])
+                go(mine & jnp.logical_not(around), lambda to: row_copy(n, p, to), to, what)
+
+                @pl.when(around)
+                def _():
+                    getattr(relay_in(n, p, to), what)()
+            else:
+                go(mine, lambda to: row_copy(n, p, to), to, what)
+
+    def relay(n, p, what):
+        if not relays:
+            return
+        for to, mine in (("down", p < 4), ("up", p >= 4)):
+            @pl.when(mine & (p % 4 >= 2) & (sy == last_hop[to][0]))
+            def _():
+                if what == "start":
+                    relay_in(n, p, to).wait_recv()
+                getattr(relay_out(n, p, to), what)()
 
     def cols_go(n, p, what):
         go(p % 2 == 0, lambda to: col_copy(n, p, to), "right", what)
@@ -77,23 +115,55 @@
     for c in copies:
         c.start()
 
-    def clear(n, c):
-        z[n, ROWS:, :] = jnp.zeros((32, COLS), bf16)
-        return c
-
-    lax.fori_loop(0, NEXP, clear, 0)
-    for n in range(NIGHTS):
-        hr[n] = jnp.zeros((2, 96, 128), bf16)
-
-    def clear_planes(p, c):
-        for n in range(NIGHTS - 1):
-            rext[n, p, 0:56, :] = jnp.zeros((56, COLS), i32)
-            rext[n, p, 64:120, :] = jnp.zeros((56, COLS), i32)
-            cext[n, p, :, 0:MC] = jnp.zeros((80, MC), i32)
-            cext[n, p, :, COLS:1024] = jnp.zeros((80, 512), i32)
-        return c
-
-    lax.fori_loop(0, PLANES, clear_planes, 0)
+    def clear_edges():
+        def halo(n, c):
+            @pl.when(jnp.logical_not(has["down"]))
+            def _():
+                z[n, 64:80, :] = jnp.zeros((16, COLS), bf16)
+
+            @pl.when(jnp.logical_not(has["up"]))
+            def _():
+                z[n, 80:96, :] = jnp.zeros((16, COLS), bf16)
+
+            return c
+
+        @pl.when(jnp.logical_not(has["up"] & has["down"]))
+        def _():
+            lax.fori_loop(0, NEXP, halo, 0)
+
+        def planes(p, c):
+            for n in range(NIGHTS - 1):
+                @pl.when(jnp.logical_not(has["up"]) & (p < 4))
+                def _():
+                    rext[n, p, 0:56, :] = jnp.zeros((56, COLS), i32)
+
+                @pl.when(jnp.logical_not(has["down"]) & (p >= 4))
+                def _():
+                    rext[n, p, 64:120, :] = jnp.zeros((56, COLS), i32)
+
+                @pl.when(jnp.logical_not(has["left"]) & (p % 2 == 0))
+                def _():
+                    cext[n, p, :, 0:MC] = jnp.zeros((72, MC), i32)
+
+                @pl.when(jnp.logical_not(has["right"]) & (p % 2 == 1))
+                def _():
+                    cext[n, p, :, COLS : COLS + MC] = jnp.zeros((72, MC), i32)
+
+            return c
+
+        @pl.when(jnp.logical_not(has["up"] & has["down"] & has["left"] & has["right"]))
+        def _():
+            lax.fori_loop(0, PLANES, planes, 0)
+            for n in range(NIGHTS):
+                @pl.when(jnp.logical_not(has["right"]))
+                def _():
+                    hr[n, 0] = jnp.zeros((96, 128), bf16)
+
+                @pl.when(jnp.logical_not(has["left"]))
+                def _():
+                    hr[n, 1] = jnp.zeros((96, 128), bf16)
+
+    clear_edges()
     taps[...] = jnp.zeros_like(taps)
     wins[...] = jnp.zeros_like(wins)
 
@@ -102,7 +172,16 @@
         @pl.when(has[to])
         def _():
             pl.semaphore_signal(barrier, inc=1, device_id=dev[to], device_id_type=MESH)
-    pl.semaphore_wait(barrier, sum(jnp.where(has[to], 1, 0) for to in dev))
+    greeted = sum(jnp.where(has[to], 1, 0) for to in dev)
+    if relays:
+        for a, b in ((mid - 1, 0), (0, mid), (mid, ny - 1), (ny - 1, mid - 1)):
+            for here, there in ((a, b), (b, a)):
+                @pl.when(sy == here)
+                def _():
+                    pl.semaphore_signal(barrier, inc=1, device_id=(there, sx), device_id_type=MESH)
+
+                greeted = greeted + jnp.where(sy == here, 1, 0)
+    pl.semaphore_wait(barrier, greeted)
 
     copies[0].wait()
     halo_go(row_halo, 0, ("up", "down"), "start")
@@ -155,6 +234,16 @@
 
     lane_row = lax.broadcasted_iota(i32, (STEP, COLS), 0)
 
+    def spread(value, rows):
+        return jnp.full((rows, COLS), value, f32)
+
+    def top(n):
+        total = jnp.float32(4.0)
+        for m in range(n + 1):
+            for e in range(EXPS):
+                total = total + gains[m, e]
+        return total * 1.0001
+
     def bits(amount, bit, shape):
         return (jnp.full(shape, amount, i32) & bit) != 0
 
@@ -162,8 +251,8 @@
         first, final = n == 0, n == NIGHTS - 1
         bit = jnp.left_shift(jnp.int32(1), p)
         if not first:
-            row_off = offs[n - 1, 2 * p]
-            col_off = offs[n - 1, 2 * p + 1]
+            row_off = offs[n - 1, p, 0]
+            col_off = offs[n - 1, p, 1]
             start = jnp.where(p % 2 == 0, MC - col_off, -col_off)
             turn = (640 - (start & 127)) % 640
 
@@ -173,13 +262,25 @@
                 x = jnp.where(bits(start, 128, (x.shape[0], 640)), x[:, 128:], x[:, :640])
                 return pltpu.roll(x, turn, 1)[:, :COLS]
 
-            own_gain = jnp.exp2(window(pl.ds(64, 8)).astype(f32) * 0.25) * (1.0 / 32766.0)
-            far_gain = jnp.exp2(window(pl.ds(72, 8)).astype(f32) * 0.25) * (1.0 / 32766.0)
-            own_gain = jnp.concatenate([own_gain, own_gain], axis=0)
-            far_gain = jnp.concatenate([far_gain, far_gain], axis=0)
-            dec = table[n, 2 * EXPS]
+            both = window(pl.ds(64, 8))
+            over = pltpu.roll(both, 4, 0)
+            low = lax.broadcasted_iota(i32, (8, COLS), 0) < 4
+
+            def gain_of(expo):
+                gain = jnp.exp2(expo.astype(f32) * 0.25) * (1.0 / 32766.0)
+                return jnp.concatenate([gain, gain], axis=0)
+
+            own_gain = gain_of(jnp.where(low, both, over))
+            far_gain = gain_of(jnp.where(low, over, both))
+            dec = top(n - 1) * (1.0 / 65535.0)
             lo = jnp.where(p < 4, row_off, 0)
             hi = jnp.where(p < 4, ROWS, ROWS + row_off)
+
+        halves = []
+        for e in range(EXPS):
+            half = band_scale / jnp.sqrt(jnp.full((8, 128), gains[n, e], f32))
+            half = jnp.concatenate([half] * (COLS // 128), axis=1)
+            halves.append(jnp.concatenate([half, half], axis=0))
 
         def step(i, peak):
             rows = pl.ds(pl.multiple_of(i * STEP, STEP), STEP)
@@ -192,8 +293,8 @@
                 flux = (packed >> 16).astype(f32) * gain
                 weight = (packed & 0xFFFF).astype(f32) * dec
             for e in range(EXPS):
-                wv = table[n, e]
-                half = table[n, EXPS + e]
+                wv = gains[n, e]
+                half = halves[e]
                 filtered = filt[n * EXPS + e, rows, :]
                 mask = masks[n * EXPS + e, rows, :]
                 mean = flux / jnp.maximum(weight, weight_floor)
@@ -217,7 +318,7 @@
             peak = jnp.maximum(peak, pltpu.roll(peak, k, 0))
         expo = jnp.ceil(4.0 * jnp.log2(jnp.maximum(peak, 1e-30)) + 0.01)
         gain = jnp.exp2(expo * -0.25) * 32766.0
-        enc = table[n, 2 * EXPS + 1]
+        enc = 65535.0 / jnp.full((8, COLS), top(n), f32)
         base = jnp.where(p < 4, 56, 0)
 
         def pack(i, c):
@@ -235,7 +336,7 @@
 
     def shift_rows(n, p):
         rows_go(n, p, "wait_recv")
-        row_off = offs[n, 2 * p]
+        row_off = offs[n, p, 0]
         start = jnp.where(p < 4, 8 + MR - row_off, -row_off)
         lanes = pl.ds(pl.multiple_of(jnp.where(p % 2 == 0, MC, 0), 128), COLS)
         x = rext[n, p]
@@ -246,12 +347,14 @@
         own = sb[n, p, pl.ds(pl.multiple_of(jnp.where(p < 4, 8, 48), 8), 8), :]
         far = rext[n, p, pl.ds(pl.multiple_of(jnp.where(p < 4, 0, 112), 8), 8), :]
         cext[n, p, 0:ROWS, lanes] = moved
-        cext[n, p, ROWS : ROWS + 8, lanes] = own
-        cext[n, p, ROWS + 8 :, lanes] = far
+        cext[n, p, ROWS:, lanes] = jnp.where(lax.broadcasted_iota(i32, (8, COLS), 0) < 4, own, far)
         cols_go(n, p, "start")
 
     def plane_at(i):
-        return (i * 5) % PLANES
+        p = ORDER[0]
+        for k in range(1, PLANES):
+            p = jnp.where(i == k, ORDER[k], p)
+        return p
 
     halo_go(row_halo, 0, ("up", "down"), "wait_recv")
     col_halo_send(0)
@@ -273,6 +376,10 @@
                     cols_go(n - 1, p, "wait_recv")
                 accumulate(n, p)
 
+                @pl.when(i >= 1)
+                def _():
+                    relay(n, plane_at(i - 1), "start")
+
                 @pl.when(i >= LAG)
                 def _():
                     shift_rows(n, plane_at(i - LAG))
@@ -282,6 +389,8 @@
 
             halo_go(col_halo, n + 1, ("left", "right"), "wait_recv")
             lax.fori_loop(0, PLANES, body, 0)
+
+            relay(n, jnp.int32(ORDER[-1]), "start")
 
             def tail(i, c):
                 shift_rows(n, plane_at(i))
@@ -312,6 +421,7 @@
         for n in range(NIGHTS - 1):
             rows_go(n, p, "wait_send")
             cols_go(n, p, "wait_send")
+            relay(n, p, "wait_send")
         return c
 
     lax.fori_loop(0, PLANES, finish, 0)
@@ -320,7 +430,7 @@
         halo_go(col_halo, n, ("left", "right"), "wait_send")
 
 
-def whole_call(table, offsets, e, kv, masks, flux, weight):
+def whole_call(gains, offsets, e, kv, masks, flux, weight):
     anywhere = pl.BlockSpec(memory_space=pl.ANY)
     smem = pl.BlockSpec(memory_space=pltpu.SMEM)
     dma = pltpu.SemaphoreType.DMA
@@ -345,40 +455,31 @@
             vm((ROWS, COLS), f32),
             vm((n, PLANES, ROWS, COLS), i32),
             vm((n, PLANES, 120, COLS), i32),
-            vm((n, PLANES, 80, 1024), i32),
+            vm((n, PLANES, 72, 1024), i32),
+            vm((n, 2, 56, COLS), i32),
             vm((PLANES, ROWS, COLS), f32),
             vm((PLANES, ROWS, COLS), f32),
             dma((4,)), dma((2, PLANES)),
             dma((NIGHTS, 2)), dma((NIGHTS, 2)), dma((NIGHTS, 2)), dma((NIGHTS, 2)),
-            dma((n, PLANES)), dma((n, PLANES)), dma((n, PLANES)), dma((n, PLANES)),
+            dma((n, PLANES)), dma((n, PLANES)), dma((n, PLANES)), dma((n, PLANES)), dma((n, 2)), dma((n, 2)),
         ],
         compiler_params=pltpu.CompilerParams(collective_id=0, has_side_effects=True, vmem_limit_bytes=60 << 20),
         name="stack",
-    )(table, offsets, e, kv, masks, flux, weight)
-
-
-def scalar_table(exposure_weights):
-    totals = 4.0 + jnp.cumsum(jnp.sum(exposure_weights, axis=1))
-    top = totals * 1.0001
-    enc = 65535.0 / top
-    dec = jnp.concatenate([jnp.ones((1,), f32), top[:-1] / 65535.0])
-    half = band_scale / jnp.sqrt(exposure_weights)
-    return jnp.concatenate([exposure_weights, half, dec[:, None], enc[:, None]], axis=1)
+    )(gains, offsets, e, kv, masks, flux, weight)
 
 
 def kernel_rows(psf_kernels):
-    k = psf_kernels.astype(f32).reshape(NEXP, KS, KS).transpose(0, 2, 1)
-    gap = jnp.zeros((NEXP, KS, 128 - KS), f32)
-    k = jnp.concatenate([k[:, :, RAD:], gap, k[:, :, :RAD]], axis=2)
-    return jnp.pad(k, ((0, 0), (0, 3), (0, 0)))
+    lane = lax.broadcasted_iota(i32, (KS, 128), 1)
+    tap = lax.broadcasted_iota(i32, (KS, 128), 0)
+    place = ((lane + RAD) % 128 == tap).astype(bf16)
+    k = jnp.einsum("neab,al->nebl", psf_kernels, place, preferred_element_type=f32)
+    return k.reshape(NEXP, KS, 128)
 
 
 def per_device(exposures, psf_kernels, clip_masks, exposure_weights, plane_offsets, flux, weight):
     e = exposures.reshape(NEXP, ROWS, COLS)
     masks = clip_masks.reshape(NEXP, ROWS, COLS)
-    table = scalar_table(exposure_weights)
-    offsets = plane_offsets.reshape(NIGHTS - 1, 2 * PLANES)
-    return tuple(whole_call(table, offsets, e, kernel_rows(psf_kernels), masks, flux, weight))
+    return tuple(whole_call(exposure_weights, plane_offsets, e, kernel_rows(psf_kernels), masks, flux, weight))
 
 
 def solution(mesh):

time: 128 us -> 125 us (0.977)
  the two profiles are of different devices: /device:TPU:22 before, /device:TPU:120 now
where the time goes in v3:
time: 125 us; the launch traced here: 124 us
  Pallas kernels  116 us (93%)
  local copies, waits for them, and re-layouts  5.95 us (5%)
    pallas_call x1, Pallas kernels, whole_call(): pl.pallas_call(whole_kernel, in_specs=[smem, smem, anywhere, pl.BlockSpec...  116 us
    unnamed x5, local copies, waits for them, and re-layouts  5.95 us

profile of v3, /device:TPU:120, one launch (start us, length us, event | category | flops | bytes accessed | tf_op | source)
XLA Modules:
  0.0 123.8 jit_solution(2374858685365776865)
XLA Ops:
  0.6 0.0 copy-start
  0.7 1.4 %copy.10.offs = s32[3,8,2]{2,1,0:T(8,128)} copy(s32[3,8,2]{1,2,0:T(2,128)} %param.11) | data formatting | bytes 384 | tf_op args[4]
  2.1 0.0 copy-done
  2.1 1.0 fusion
  3.1 116.1 %stack.1 = (f32[8,64,512]{2,1,0:T(8,128)}, f32[8,64,512]{2,1,0:T(8,128)}) custom-call(f32[4,8]{1,0:T(4,128)} %gains.1, s32[3,8,2]{2,1,0:T(8,128)} %copy.10.offs, bf16[32,64,512]{2,1,0:T(8,128)(2,1)} %bitcast.11, f32[32,21,128]{2,1,0:T(8,128)} %bitcast.12, s32[32,64,512]{2,1,0:T(8,128)} %bitcast.10, f32[8,64,512]{2,1,0:T(8,128)} %flux_hbm.1, ...), custom_call_target="tpu_custom_call" | custom-call | tf_op jit(solution)/shard_map/stack/pallas_call | solution.py:439
  119.2 2.3 %copy.16 = f32[8,64,512]{2,1,0:T(8,128)} copy(f32[8,64,512]{2,1,0:T(8,128)} %get-tuple-element.6) | data formatting | bytes 2097152
  121.5 2.3 %copy.17 = f32[8,64,512]{2,1,0:T(8,128)} copy(f32[8,64,512]{2,1,0:T(8,128)} %get-tuple-element.7) | data formatting | bytes 2097152
  (2 shorter events, 0.0 us)
Async XLA Ops:
  0.6 1.5 %copy-start = (bf16[4,8,21,21]{3,1,2,0:T(8,128)(2,1)S(1)}, bf16[4,8,21,21]{3,1,2,0:T(8,128)(2,1)}, u32[]{:S(2)}) copy-start(bf16[4,8,21,21]{3,1,2,0:T(8,128)(2,1)} %param.8) | copy-start | bytes 84676

commit v4 on v3

--- a/solution.py
+++ b/solution.py
@@ -13,7 +13,7 @@
 PLANES, NIGHTS, EXPS, KS, RAD = 8, 4, 8, 21, 10
 NEXP = NIGHTS * EXPS
 STEP = 16
-LAG = 3
+LAG = 6
 ORDER = (2, 7, 0, 5, 3, 6, 1, 4)
 MESH = pl.DeviceIdType.MESH
 
@@ -26,7 +26,7 @@
     has = {"up": sy > 0, "down": sy < ny - 1, "left": sx > 0, "right": sx < nx - 1}
     dev = {"up": (sy - 1, sx), "down": (sy + 1, sx), "left": (sy, sx - 1), "right": (sy, sx + 1)}
     mid = ny // 2
-    relays = ny == 8
+    relays = False
     first_hop = {"down": (mid - 1, 0), "up": (mid, ny - 1)}
     last_hop = {"down": (0, mid), "up": (ny - 1, mid - 1)}
     back = {"up": "down", "down": "up", "left": "right", "right": "left"}

time: 125 us -> 99.4 us (0.80)
  Pallas kernels: 116 us -> 90.5 us
    pallas_call x1, Pallas kernels: 116 us -> 90.5 us  [whole_call(): pl.pallas_call(whole_kernel, in_specs=[smem, smem, anywhere, pl.BlockSpec...]
where the time goes in v4:
time: 99.4 us; the launch traced here: 98.2 us
  Pallas kernels  90.5 us (91%)
  local copies, waits for them, and re-layouts  5.95 us (6%)
  matrix products  1 us (1%)
    pallas_call x1, Pallas kernels, whole_call(): pl.pallas_call(whole_kernel, in_specs=[smem, smem, anywhere, pl.BlockSpec...  90.5 us
    unnamed x5, local copies, waits for them, and re-layouts  5.95 us

profile of v4, /device:TPU:120, one launch (start us, length us, event | category | flops | bytes accessed | tf_op | source)
XLA Modules:
  0.0 98.2 jit_solution(12624972899506419348)
XLA Ops:
  0.6 0.0 copy-start
  0.7 1.4 %copy.10.offs = s32[3,8,2]{2,1,0:T(8,128)} copy(s32[3,8,2]{1,2,0:T(2,128)} %param.11) | data formatting | bytes 384 | tf_op args[4]
  2.1 0.0 copy-done
  2.1 1.0 %fusion = f32[128,4,8,21]{0,3,2,1:T(8,128)} fusion(bf16[4,8,21,21]{3,1,2,0:T(8,128)(2,1)S(1)} %copy-done, s32[128]{0:T(128)S(1)} %get-tuple-element.2, s32[128]{0:T(128)S(1)} %get-tuple-element.3, pred[128]{0:T(512)(128)(4,1)S(1)} %compare_and_fusion), kind=kOutput, calls=%fused_computation | convolution fusion | flops 3618048 | bytes 373440 | tf_op jit(solution)/shard_map/neab,al->nebl/dot_general | solution.py:475
  3.1 90.5 %stack.1 = (f32[8,64,512]{2,1,0:T(8,128)}, f32[8,64,512]{2,1,0:T(8,128)}) custom-call(f32[4,8]{1,0:T(4,128)} %gains.1, s32[3,8,2]{2,1,0:T(8,128)} %copy.10.offs, bf16[32,64,512]{2,1,0:T(8,128)(2,1)} %bitcast.11, f32[32,21,128]{2,1,0:T(8,128)} %bitcast.12, s32[32,64,512]{2,1,0:T(8,128)} %bitcast.10, f32[8,64,512]{2,1,0:T(8,128)} %flux_hbm.1, ...), custom_call_target="tpu_custom_call" | custom-call | tf_op jit(solution)/shard_map/stack/pallas_call | solution.py:439
  93.6 2.3 %copy.16 = f32[8,64,512]{2,1,0:T(8,128)} copy(f32[8,64,512]{2,1,0:T(8,128)} %get-tuple-element.6) | data formatting | bytes 2097152
  95.9 2.3 %copy.17 = f32[8,64,512]{2,1,0:T(8,128)} copy(f32[8,64,512]{2,1,0:T(8,128)} %get-tuple-element.7) | data formatting | bytes 2097152
  (2 shorter events, 0.0 us)
Async XLA Ops:
  0.6 1.5 %copy-start = (bf16[4,8,21,21]{3,1,2,0:T(8,128)(2,1)S(1)}, bf16[4,8,21,21]{3,1,2,0:T(8,128)(2,1)}, u32[]{:S(2)}) copy-start(bf16[4,8,21,21]{3,1,2,0:T(8,128)(2,1)} %param.8) | copy-start | bytes 84676
